TPU v7x, 32 devices: a whole 2x2x4 slice. The times are simulated.
32 devices in a mesh: row: 4 (over y, x), col: 8 (over z, core).
Axes of the slice: x: 2, y: 2, z: 4, core: 2. Of those that a mesh axis runs over, the one named last changes fastest.
Arguments:
- tokens: bfloat16 [4096, 2048], P(('row', 'col')), may hold values from -6 to 6
- cotangent: bfloat16 [4096, 2048], P(('row', 'col')), may hold values from -6 to 6
- permutation: int32 [4096], replicated, may hold values from 0 to 4095, as said below
- lengths: int32 [8, 4], P('col'), may hold values from 1 to 384, 512 in all within a row
- attention_gain: bfloat16 [2048], replicated, may hold values from 0.5 to 1.5
- query_projection_weight: bfloat16 [2048, 2048], P('col', 'row'), may hold values from -0.125 to 0.125
- key_value_weight: bfloat16 [2048, 512], P('col'), may hold values from -0.125 to 0.125
- projection_adapter_first: bfloat16 [2048, 256], P('col'), may hold values from -0.125 to 0.125
- query_adapter_second: bfloat16 [256, 2048], P(None, 'row'), may hold values from -0.375 to 0.375
- key_value_second: bfloat16 [256, 512], replicated, may hold values from -0.375 to 0.375
- output_projection_weight: bfloat16 [2048, 2048], P('row', 'col'), may hold values from -2 to 2
- output_adapter_first: bfloat16 [2048, 256], P('row'), may hold values from -2 to 2
- output_adapter_second: bfloat16 [256, 2048], replicated, may hold values from -0.375 to 0.375
- hidden_gain: bfloat16 [2048], replicated, may hold values from 0.5 to 1.5
- gate_up_weight: bfloat16 [2048, 2, 16384], P('col', None, 'row'), may hold values from -0.125 to 0.125
- widen_adapter_first: bfloat16 [2048, 256], P('col'), may hold values from -0.125 to 0.125
- widen_adapter_second: bfloat16 [256, 2, 16384], P(None, None, 'row'), may hold values from -0.375 to 0.375
- down_projection_weight: bfloat16 [16384, 2048], P('row', 'col'), may hold values from -0.046875 to 0.046875
- narrow_adapter_first: bfloat16 [16384, 256], P('row'), may hold values from -0.046875 to 0.046875
- narrow_adapter_second: bfloat16 [256, 2048], replicated, may hold values from -0.375 to 0.375
Outputs:
- block_output: bfloat16 [4096, 2048], P(('row', 'col'))
- grad_tokens: bfloat16 [4096, 2048], P(('row', 'col'))
- grad_attention_gain: float32 [2048], replicated
- grad_query_weight: float32 [2048, 2048], P('col', 'row')
- grad_keyval_weight: float32 [2048, 512], P('col')
- projection_first_gradient: float32 [2048, 256], P('col')
- query_second_gradient: float32 [256, 2048], P(None, 'row')
- key_value_second_gradient: float32 [256, 512], replicated
- grad_output_weight: float32 [2048, 2048], P('row', 'col')
- output_first_gradient: float32 [2048, 256], P('row')
- output_second_gradient: float32 [256, 2048], replicated
- grad_hidden_gain: float32 [2048], replicated
- grad_expand_weight: float32 [2048, 2, 16384], P('col', None, 'row')
- widen_first_gradient: float32 [2048, 256], P('col')
- widen_second_gradient: float32 [256, 2, 16384], P(None, None, 'row')
- grad_shrink_weight: float32 [16384, 2048], P('row', 'col')
- narrow_first_gradient: float32 [16384, 256], P('row')
- narrow_second_gradient: float32 [256, 2048], replicated
Inputs may be any that keep to these rules, and one draw needn't show every extreme that they name: `permutation`: packed position (c * 512) + r * 128 + s, for token group c, row device r and slot s < 128, takes a token from the given positions (r * 8 + s // 16) * 128 to that plus 128 - 1; every given position appears once. `lengths`: each row sums to 512.
All inputs are finite; a program needn't handle non-finite values.
Results may differ from a plain program's by a relative error of at most 0.025.
Values may be sent and summed in bfloat16 or wider, within the bound.
No kernel may reach another device: no remote copies, remote signals or barrier semaphores. Data moves between devices by JAX's collectives and lax.ppermute only.
A program may use at most 320 MiB of HBM per device.

v0:
```python
import math

import jax
import jax.numpy as jnp
from jax import lax
from jax.sharding import PartitionSpec as P

EPSILON = 1e-06
MASKED = -1e30


def shortened(value):

    def short(part):
        return part.astype(jnp.bfloat16) if part.dtype == jnp.float32 else part

    return jax.tree.map(short, value)


def matrix_product(left_op, right_op):
    return jnp.dot(left_op, right_op, preferred_element_type=jnp.float32)


def inner_row_count(left_op, right_op):
    return lax.dot_general(
        left_op, right_op, (((0,), (0,)), ((), ())), preferred_element_type=jnp.float32
    )


def inner_column_count(left_op, right_op):
    return lax.dot_general(
        left_op, right_op, (((1,), (1,)), ((), ())), preferred_element_type=jnp.float32
    )


def normalize(values, norm_gain):
    inverse = lax.rsqrt(jnp.mean(values * values, axis=1, keepdims=True) + EPSILON)
    return values * inverse * norm_gain


def rotary_tables(positions, head_dim):
    half_dim = head_dim // 2
    inverse_freq = jnp.exp(
        jnp.arange(half_dim, dtype=jnp.float32) * (-2.0 * math.log(10000.0) / head_dim)
    )
    angles = positions.astype(jnp.float32)[:, None] * inverse_freq[None, :]
    return (jnp.cos(angles), jnp.sin(angles))


def rotate(values, cosine, sine_table):
    half_dim = values.shape[-1] // 2
    first_half = values[..., :half_dim]
    second_half = values[..., half_dim:]
    return jnp.concatenate(
        [
            first_half * cosine - second_half * sine_table,
            second_half * cosine + first_half * sine_table,
        ],
        axis=-1,
    )


def group_layout(lengths, group_size):
    seq_ends = jnp.cumsum(lengths, axis=-1)
    starts = seq_ends - lengths
    places = jnp.arange(group_size, dtype=jnp.int32)
    segment = jnp.sum((places[:, None] >= seq_ends[None, :]).astype(jnp.int32), axis=-1)
    chosen = segment[:, None] == jnp.arange(lengths.shape[0], dtype=jnp.int32)[None, :]
    offsets = jnp.sum(jnp.where(chosen, starts[None, :], 0), axis=-1)
    return (segment, places - offsets)


def allowed_mask(segment, row_start, block_rows):
    places = jnp.arange(segment.shape[0])
    query_seg = lax.dynamic_slice_in_dim(segment, row_start, block_rows, 0)
    query_pos = row_start + jnp.arange(block_rows)
    return (query_seg[:, None] == segment[None, :]) & (places[None, :] <= query_pos[:, None])


def attend(queries, key_rows, value_rows, segment):
    group_size = key_rows.shape[0]
    block_rows = min(512, group_size)

    def one_block(block_id):
        row_start = block_id * block_rows
        query_block = lax.dynamic_slice_in_dim(queries, row_start, block_rows, 0)
        allowed = allowed_mask(segment, row_start, block_rows)
        scores = jnp.einsum(
            "qhd,kd->hqk", query_block, key_rows, preferred_element_type=jnp.float32
        )
        scores = jnp.where(allowed[None], scores, MASKED)
        maximum = jnp.max(scores, axis=2, keepdims=True)
        exponent = jnp.exp(scores - maximum)
        denominator = jnp.sum(exponent, axis=2, keepdims=True)
        weights_low = (exponent / denominator).astype(jnp.bfloat16)
        mixed_block = jnp.einsum(
            "hqk,kd->qhd", weights_low, value_rows, preferred_element_type=jnp.float32
        )
        return (mixed_block, maximum + jnp.log(denominator))

    mixed_blocks, log_total = lax.map(one_block, jnp.arange(group_size // block_rows))
    return (mixed_blocks.reshape(group_size, queries.shape[1], queries.shape[2]), log_total)


def attend_back(queries, key_rows, value_rows, segment, log_total, grad_mixed):
    group_size = key_rows.shape[0]
    block_rows = min(512, group_size)

    def one_block(carried, block_id):
        grad_keys, grad_values = carried
        row_start = block_id * block_rows
        query_block = lax.dynamic_slice_in_dim(queries, row_start, block_rows, 0)
        grad_block = lax.dynamic_slice_in_dim(grad_mixed, row_start, block_rows, 0)
        allowed = allowed_mask(segment, row_start, block_rows)
        scores = jnp.einsum(
            "qhd,kd->hqk", query_block, key_rows, preferred_element_type=jnp.float32
        )
        scores = jnp.where(allowed[None], scores, MASKED)
        prob_rows = jnp.exp(scores - log_total[block_id])
        prob_low = prob_rows.astype(jnp.bfloat16)
        grad_probs = jnp.einsum(
            "qhd,kd->hqk", grad_block, value_rows, preferred_element_type=jnp.float32
        )
        shared = jnp.sum(prob_rows * grad_probs, axis=2, keepdims=True)
        grad_scores = (prob_rows * (grad_probs - shared)).astype(jnp.bfloat16)
        grad_query = jnp.einsum(
            "hqk,kd->qhd", grad_scores, key_rows, preferred_element_type=jnp.float32
        )
        grad_keys = grad_keys + jnp.einsum(
            "hqk,qhd->kd", grad_scores, query_block, preferred_element_type=jnp.float32
        )
        grad_values = grad_values + jnp.einsum(
            "hqk,qhd->kd", prob_low, grad_block, preferred_element_type=jnp.float32
        )
        return ((grad_keys, grad_values), grad_query)

    zeros_kv = jnp.zeros(key_rows.shape, jnp.float32)
    (grad_keys, grad_values), grad_query = lax.scan(
        one_block, (zeros_kv, zeros_kv), jnp.arange(group_size // block_rows)
    )
    return (grad_query.reshape(queries.shape), grad_keys, grad_values)


def gather_rows(values):
    return lax.all_gather(values, "row", axis=0, tiled=True)


def reduce_rows(activations, weight, adapter):

    def partial_term(row_start, take_count):
        return jnp.concatenate(
            [matrix_product(activations, weight), matrix_product(activations, adapter)], axis=1
        )

    return lax.psum_scatter(
        partial_term(
            jnp.int32(0), activations.shape[0] // lax.axis_size("row") * lax.axis_size("row")
        ),
        "row",
        scatter_dimension=0,
        tiled=True,
    )


def collected_gradients(incoming_gradient, adapter_gradient):
    return (
        lax.all_gather(incoming_gradient, "row", axis=0, tiled=True),
        lax.all_gather(adapter_gradient, "row", axis=0, tiled=True),
    )


def reduce_grads(incoming_gradient, weight):

    def partial_term(row_start, take_count):
        return inner_column_count(incoming_gradient, weight)

    return lax.psum_scatter(
        partial_term(
            jnp.int32(0), incoming_gradient.shape[0] // lax.axis_size("row") * lax.axis_size("row")
        ).astype(jnp.bfloat16),
        "row",
        scatter_dimension=0,
        tiled=True,
    ).astype(jnp.float32)


def total_row_count(values):
    return jax.tree.map(lambda part: part.astype(jnp.float32), lax.psum(shortened(values), "row"))


def per_device(
    tokens,
    cotangent,
    permutation,
    lengths,
    attention_gain,
    query_projection_weight,
    key_value_weight,
    projection_adapter_first,
    query_adapter_second,
    key_value_second,
    output_projection_weight,
    output_adapter_first,
    output_adapter_second,
    hidden_gain,
    gate_up_weight,
    widen_adapter_first,
    widen_adapter_second,
    down_projection_weight,
    narrow_adapter_first,
    narrow_adapter_second,
):
    token_count = tokens.shape[0]
    hidden_width = tokens.shape[1]
    row_count = lax.axis_size("row")
    col_count = lax.axis_size("col")
    row_index = lax.axis_index("row")
    col_index = lax.axis_index("col")
    group_size = token_count * row_count
    head_dim = key_value_weight.shape[1] // 2
    rank_size = projection_adapter_first.shape[1]
    width_share = token_count // col_count
    local_row_values = row_index * token_count
    targets = jnp.arange(col_count, dtype=jnp.int32)[:, None]
    slot_ids = jnp.arange(width_share, dtype=jnp.int32)[None, :]
    packed = (targets * row_count + row_index) * token_count + col_index * width_share + slot_ids
    sources = (
        jnp.take(permutation, packed.reshape(-1))
        - (row_index * col_count + col_index) * token_count
    )
    dealt_in, dealt_grad = (
        lax.all_to_all(
            tokens[sources].reshape(col_count, width_share, hidden_width),
            "col",
            split_axis=0,
            concat_axis=0,
            tiled=True,
        ),
        lax.all_to_all(
            cotangent[sources].reshape(col_count, width_share, hidden_width),
            "col",
            split_axis=0,
            concat_axis=0,
            tiled=True,
        ),
    )
    residual_stream = dealt_in.reshape(token_count, hidden_width).astype(jnp.float32)
    output_gradient_rows = dealt_grad.reshape(token_count, hidden_width)
    segment, positions = group_layout(lengths[0], group_size)
    cosine, sine_table = rotary_tables(positions, head_dim)
    (
        query_complete,
        key_value_complete,
        projection_first_complete,
        expand_full,
        widen_adapter_first_whole,
        output_complete,
        narrow_complete,
    ) = (
        lax.all_gather(query_projection_weight, "col", axis=0, tiled=True),
        lax.all_gather(key_value_weight, "col", axis=0, tiled=True),
        lax.all_gather(projection_adapter_first, "col", axis=0, tiled=True),
        lax.all_gather(gate_up_weight, "col", axis=0, tiled=True),
        lax.all_gather(widen_adapter_first, "col", axis=0, tiled=True),
        lax.all_gather(output_projection_weight, "col", axis=1, tiled=True),
        lax.all_gather(down_projection_weight, "col", axis=1, tiled=True),
    )
    attn_gain = attention_gain.astype(jnp.float32)
    collected_input_rows = gather_rows(normalize(residual_stream, attn_gain).astype(jnp.bfloat16))
    adapter_projection = matrix_product(collected_input_rows, projection_first_complete).astype(
        jnp.bfloat16
    )
    query_linear = matrix_product(collected_input_rows, query_complete) + matrix_product(
        adapter_projection, query_adapter_second
    )
    key_value_linear = matrix_product(collected_input_rows, key_value_complete) + matrix_product(
        adapter_projection, key_value_second
    )
    heads_local = query_linear.shape[1] // head_dim
    query_scale = head_dim ** (-0.5)
    queries = (
        rotate(
            query_linear.reshape(group_size, heads_local, head_dim),
            cosine[:, None, :],
            sine_table[:, None, :],
        )
        * query_scale
    ).astype(jnp.bfloat16)
    key_rows = rotate(key_value_linear[:, :head_dim], cosine, sine_table).astype(jnp.bfloat16)
    value_rows = key_value_linear[:, head_dim:].astype(jnp.bfloat16)
    mixed_heads, log_total = attend(queries, key_rows, value_rows, segment)
    mixed_reduced_rank = mixed_heads.reshape(group_size, -1).astype(jnp.bfloat16)
    attention_pieces_list = reduce_rows(mixed_reduced_rank, output_complete, output_adapter_first)
    adapter_output = attention_pieces_list[:, hidden_width:].astype(jnp.bfloat16)
    hidden_state = (
        residual_stream
        + attention_pieces_list[:, :hidden_width]
        + matrix_product(adapter_output, output_adapter_second)
    )
    ffn_gain = hidden_gain.astype(jnp.float32)
    collected_middle_rows = gather_rows(normalize(hidden_state, ffn_gain).astype(jnp.bfloat16))
    widen_weight_flattened = expand_full.reshape(expand_full.shape[0], -1)
    up_flattened = widen_adapter_second.reshape(rank_size, -1)
    adapter_middle = matrix_product(collected_middle_rows, widen_adapter_first_whole).astype(
        jnp.bfloat16
    )
    gate_up_product = matrix_product(
        collected_middle_rows, widen_weight_flattened
    ) + matrix_product(adapter_middle, up_flattened)
    unit_count = gate_up_product.shape[1] // 2
    gate_portion = gate_up_product[:, :unit_count]
    up_portion = gate_up_product[:, unit_count:]
    activated_hidden = (jax.nn.gelu(gate_portion, approximate=True) * up_portion).astype(
        jnp.bfloat16
    )
    feedforward_pieces = reduce_rows(activated_hidden, narrow_complete, narrow_adapter_first)
    adapter_final = feedforward_pieces[:, hidden_width:].astype(jnp.bfloat16)
    block_result_rows = (
        hidden_state
        + feedforward_pieces[:, :hidden_width]
        + matrix_product(adapter_final, narrow_adapter_second)
    )
    (
        query_complete,
        key_value_complete,
        projection_first_complete,
        expand_full,
        widen_adapter_first_whole,
        output_complete,
        narrow_complete,
    ) = (
        lax.all_gather(query_projection_weight, "col", axis=0, tiled=True),
        lax.all_gather(key_value_weight, "col", axis=0, tiled=True),
        lax.all_gather(projection_adapter_first, "col", axis=0, tiled=True),
        lax.all_gather(gate_up_weight, "col", axis=0, tiled=True),
        lax.all_gather(widen_adapter_first, "col", axis=0, tiled=True),
        lax.all_gather(output_projection_weight, "col", axis=1, tiled=True),
        lax.all_gather(down_projection_weight, "col", axis=1, tiled=True),
    )
    widen_weight_flattened = expand_full.reshape(expand_full.shape[0], -1)
    adapter_final_gradient = inner_column_count(output_gradient_rows, narrow_adapter_second).astype(
        jnp.bfloat16
    )
    narrow_second_gradient = inner_row_count(adapter_final, output_gradient_rows)
    gradient_row_values, adapter_row_values = collected_gradients(
        output_gradient_rows, adapter_final_gradient
    )
    grad_shrink = inner_row_count(activated_hidden, gradient_row_values)
    narrow_first_gradient = inner_row_count(activated_hidden, adapter_row_values)
    activated_gradient = inner_column_count(
        gradient_row_values, narrow_complete
    ) + inner_column_count(adapter_row_values, narrow_adapter_first)
    _, gelu_back = jax.vjp(
        lambda gate_in, up_in: jax.nn.gelu(gate_in, approximate=True) * up_in,
        gate_portion,
        up_portion,
    )
    grad_gate, grad_up = gelu_back(activated_gradient)
    gate_up_gradient = jnp.concatenate([grad_gate, grad_up], axis=1).astype(jnp.bfloat16)
    (adapter_middle_sum,) = total_row_count((inner_column_count(gate_up_gradient, up_flattened),))
    adapter_middle_gradient = adapter_middle_sum.astype(jnp.bfloat16)
    widen_second_gradient = inner_row_count(adapter_middle, gate_up_gradient)
    grad_expand = inner_row_count(collected_middle_rows, gate_up_gradient)
    widen_first_gradient = inner_row_count(collected_middle_rows, adapter_middle_gradient)
    local_middle = lax.dynamic_slice_in_dim(
        adapter_middle_gradient, local_row_values, token_count, 0
    )
    grad_normed_mid = reduce_grads(gate_up_gradient, widen_weight_flattened) + inner_column_count(
        local_middle, widen_adapter_first_whole
    )
    _, norm_back_mid = jax.vjp(normalize, hidden_state, ffn_gain)
    grad_hidden_norm, grad_ffn_gain = norm_back_mid(grad_normed_mid)
    grad_hidden = output_gradient_rows.astype(jnp.float32) + grad_hidden_norm
    attention_gradient = grad_hidden.astype(jnp.bfloat16)
    adapter_output_gradient = inner_column_count(attention_gradient, output_adapter_second).astype(
        jnp.bfloat16
    )
    output_second_gradient = inner_row_count(adapter_output, attention_gradient)
    attention_row_outputs, attention_adapter_rows = collected_gradients(
        attention_gradient, adapter_output_gradient
    )
    grad_output = inner_row_count(mixed_reduced_rank, attention_row_outputs)
    output_first_gradient = inner_row_count(mixed_reduced_rank, attention_adapter_rows)
    grad_mixed = (
        inner_column_count(attention_row_outputs, output_complete)
        + inner_column_count(attention_adapter_rows, output_adapter_first)
    ).astype(jnp.bfloat16)
    grad_query_rot, grad_key_rot, grad_value = attend_back(
        queries,
        key_rows,
        value_rows,
        segment,
        log_total,
        grad_mixed.reshape(group_size, heads_local, head_dim),
    )
    query_linear_gradient = (
        (rotate(grad_query_rot, cosine[:, None, :], -sine_table[:, None, :]) * query_scale)
        .reshape(group_size, -1)
        .astype(jnp.bfloat16)
    )
    key_column_total, value_column_total, adapter_projection_portion = total_row_count(
        (grad_key_rot, grad_value, inner_column_count(query_linear_gradient, query_adapter_second))
    )
    key_value_gradient = jnp.concatenate(
        [rotate(key_column_total, cosine, -sine_table), value_column_total], axis=1
    ).astype(jnp.bfloat16)
    adapter_projection_gradient = (
        adapter_projection_portion + inner_column_count(key_value_gradient, key_value_second)
    ).astype(jnp.bfloat16)
    query_second_gradient = inner_row_count(adapter_projection, query_linear_gradient)
    key_value_second_gradient = inner_row_count(adapter_projection, key_value_gradient)
    grad_query = inner_row_count(collected_input_rows, query_linear_gradient)
    grad_keyval_weight = inner_row_count(collected_input_rows, key_value_gradient)
    projection_first_gradient = inner_row_count(collected_input_rows, adapter_projection_gradient)
    own_keyval = lax.dynamic_slice_in_dim(key_value_gradient, local_row_values, token_count, 0)
    local_adapter = lax.dynamic_slice_in_dim(
        adapter_projection_gradient, local_row_values, token_count, 0
    )
    grad_normed_in = (
        reduce_grads(query_linear_gradient, query_complete)
        + inner_column_count(own_keyval, key_value_complete)
        + inner_column_count(local_adapter, projection_first_complete)
    )
    _, norm_back_in = jax.vjp(normalize, residual_stream, attn_gain)
    grad_in_norm, grad_attn_gain = norm_back_in(grad_normed_in)
    grad_packed = grad_hidden + grad_in_norm
    (
        grad_query_weight,
        grad_keyval_owned,
        grad_qkv_owned,
        grad_expand_weight,
        grad_expand_owned,
        grad_output_weight,
        grad_shrink_weight,
    ) = (
        lax.psum_scatter(
            grad_query.astype(jnp.bfloat16), "col", scatter_dimension=0, tiled=True
        ).astype(jnp.float32),
        lax.psum_scatter(
            grad_keyval_weight.astype(jnp.bfloat16), "col", scatter_dimension=0, tiled=True
        ).astype(jnp.float32),
        lax.psum_scatter(
            projection_first_gradient.astype(jnp.bfloat16), "col", scatter_dimension=0, tiled=True
        ).astype(jnp.float32),
        lax.psum_scatter(
            grad_expand.reshape(grad_expand.shape[0], 2, -1).astype(jnp.bfloat16),
            "col",
            scatter_dimension=0,
            tiled=True,
        ).astype(jnp.float32),
        lax.psum_scatter(
            widen_first_gradient.astype(jnp.bfloat16), "col", scatter_dimension=0, tiled=True
        ).astype(jnp.float32),
        lax.psum_scatter(
            grad_output.astype(jnp.bfloat16), "col", scatter_dimension=1, tiled=True
        ).astype(jnp.float32),
        lax.psum_scatter(
            grad_shrink.astype(jnp.bfloat16), "col", scatter_dimension=1, tiled=True
        ).astype(jnp.float32),
    )
    (
        grad_query_summed,
        grad_keyval_summed,
        grad_expand_summed,
        grad_output_down_sum,
        grad_shrink_down_sum,
    ) = (
        lax.psum(query_second_gradient.astype(jnp.bfloat16), "col").astype(jnp.float32),
        lax.psum(key_value_second_gradient.astype(jnp.bfloat16), "col").astype(jnp.float32),
        lax.psum(
            widen_second_gradient.reshape(rank_size, 2, -1).astype(jnp.bfloat16), "col"
        ).astype(jnp.float32),
        lax.psum(output_first_gradient.astype(jnp.bfloat16), "col").astype(jnp.float32),
        lax.psum(narrow_first_gradient.astype(jnp.bfloat16), "col").astype(jnp.float32),
    )
    grad_output_up_sum, grad_shrink_up_sum, grad_attn_gain_sum, grad_ffn_gain_sum = lax.psum(
        (output_second_gradient, narrow_second_gradient, grad_attn_gain, grad_ffn_gain),
        ("row", "col"),
    )
    back_out, back_grad = (
        lax.all_to_all(
            block_result_rows.astype(jnp.bfloat16).reshape(col_count, width_share, hidden_width),
            "col",
            split_axis=0,
            concat_axis=0,
            tiled=True,
        ),
        lax.all_to_all(
            grad_packed.astype(jnp.bfloat16).reshape(col_count, width_share, hidden_width),
            "col",
            split_axis=0,
            concat_axis=0,
            tiled=True,
        ),
    )
    inverse = jnp.argsort(sources)
    final_out = back_out.reshape(token_count, hidden_width)[inverse]
    final_grad = back_grad.reshape(token_count, hidden_width)[inverse]
    return (
        final_out,
        final_grad,
        grad_attn_gain_sum,
        grad_query_weight,
        grad_keyval_owned,
        grad_qkv_owned,
        grad_query_summed,
        grad_keyval_summed,
        grad_output_weight,
        grad_output_down_sum,
        grad_output_up_sum,
        grad_ffn_gain_sum,
        grad_expand_weight,
        grad_expand_owned,
        grad_expand_summed,
        grad_shrink_weight,
        grad_shrink_down_sum,
        grad_shrink_up_sum,
    )


def solution(mesh):
    return jax.shard_map(
        per_device,
        mesh=mesh,
        in_specs=(
            P(("row", "col"), None),
            P(("row", "col"), None),
            P(),
            P("col", None),
            P(),
            P("col", "row"),
            P("col", None),
            P("col", None),
            P(None, "row"),
            P(),
            P("row", "col"),
            P("row", None),
            P(),
            P(),
            P("col", None, "row"),
            P("col", None),
            P(None, None, "row"),
            P("row", "col"),
            P("row", None),
            P(),
        ),
        out_specs=(
            P(("row", "col"), None),
            P(("row", "col"), None),
            P(),
            P("col", "row"),
            P("col", None),
            P("col", None),
            P(None, "row"),
            P(),
            P("row", "col"),
            P("row", None),
            P(),
            P(),
            P("col", None, "row"),
            P("col", None),
            P(None, None, "row"),
            P("row", "col"),
            P("row", None),
            P(),
        ),
        check_vma=False,
    )
```

profile of v0, /device:TPU:0, one launch (start us, length us, event | category | flops | bytes accessed | tf_op | source)
XLA Modules:
  0.0 2421.3 jit_solution(16279134705790148020)
XLA Ops:
  19.6 23.5 all-to-all-done
  47.0 32.7 %all-gather.12.cloned.1.call-done = bf16[512,2048]{1,0:T(8,128)(2,1)} async-done(((bf16[128,2048]{1,0:T(8,128)(2,1)}), bf16[512,2048]{1,0:T(8,128)(2,1)}) %all-gather.12.cloned.1.call-update) | async-done | bytes 2097168 | tf_op jit(solution)/shard_map/all_gather | solution.py:145
  82.3 28.2 %all-gather.18.cloned.1.call-done = bf16[2048,512]{1,0:T(8,128)(2,1)} async-done(((bf16[256,512]{1,0:T(8,128)(2,1)}), bf16[2048,512]{1,0:T(8,128)(2,1)}) %all-gather.18.cloned.1.call-update) | async-done | bytes 2097168 | tf_op jit(solution)/shard_map/all_gather | solution.py:260
  119.5 21.0 all-gather.14.cloned.1.call-done
  178.4 55.3 %reduce-scatter.11.cloned.1.call-done = f32[128,2304]{1,0:T(8,128)} async-done(((f32[512,2304]{1,0:T(8,128)}), f32[128,2304]{1,0:T(8,128)}) %reduce-scatter.11.cloned.1.call-update) | async-done | bytes 1179664 | tf_op jit(solution)/shard_map/reduce_scatter | solution.py:155
  239.7 26.4 %all_to_all.20 = bf16[8,16,2048]{2,1,0:T(8,128)(2,1)} all-to-all(bf16[8,16,2048]{2,1,0:T(8,128)(2,1)S(1)} %bitcast.203), channel_id=1, replica_groups=mesh['row'=4,'col'=8] {'col'}, dimensions={0} | all-to-all | bytes 1048576 | tf_op jit(solution)/shard_map/all_to_all | solution.py:239
  307.1 287.7 %all-gather.24.cloned.1.call-done = bf16[2048,2,4096]{2,1,0:T(2,128)(2,1)} async-done(((bf16[256,2,4096]{2,1,0:T(2,128)(2,1)}), bf16[2048,2,4096]{2,1,0:T(2,128)(2,1)}) %all-gather.24.cloned.1.call-update) | async-done | bytes 33554448 | tf_op jit(solution)/shard_map/all_gather | solution.py:263
  594.8 29.9 %copy.124 = bf16[256,8,2,4096]{3,1,2,0:T(8,128)(2,1)} copy(bf16[256,8,2,4096]{3,2,1,0:T(2,128)(2,1)} %bitcast.183) | data formatting | bytes 67108864
  624.6 27.2 %fusion.86 = f32[512,8192]{1,0:T(8,128)} fusion(bf16[512,2048]{1,0:T(8,128)(2,1)} %all-gather.22.cloned.1.call-done, bf16[2048,8192]{1,0:T(8,128)(2,1)} %bitcast.184), kind=kOutput, calls=%fused_computation.184 | convolution fusion | flops 17179869184 | bytes 52428800 | tf_op jit(solution)/shard_map/dot_general | solution.py:21
  667.2 116.1 %all-gather.28.cloned.1.call-done = bf16[4096,2048]{1,0:T(8,128)(2,1)} async-done(((bf16[4096,256]{1,0:T(8,128)(2,1)}), bf16[4096,2048]{1,0:T(8,128)(2,1)}) %all-gather.28.cloned.1.call-update) | async-done | bytes 16777232 | tf_op jit(solution)/shard_map/all_gather | solution.py:266
  783.3 25.2 %fusion.6 = (bf16[512,4096]{1,0:T(8,128)(2,1)}, bf16[512,4096]{1,0:T(8,128)(2,1)}, bf16[512,4096]{1,0:T(8,128)(2,1)}) fusion(f32[512,8192]{1,0:T(8,128)} %convolution_add_fusion, f32[512,4096]{1,0:T(8,128)} %fusion.89, bf16[512,2048]{1,0:T(8,128)(2,1)} %all-gather.30.cloned.1.call-done, bf16[4096,2048]{1,0:T(8,128)(2,1)} %all-gather.28.cloned.1.call-done), kind=kOutput, calls=%fused_computation.17 | convolution fusion | flops 8646557696 | bytes 56623104 | tf_op jit(solution)/shard_map/dot_general | solution.py:31
  816.4 24.9 %convolution_convert_fusion.4 = bf16[512,2048]{1,0:T(8,128)(2,1)} fusion(bf16[2048,8192]{1,0:T(8,128)(2,1)} %bitcast.185, bf16[512,4096]{1,0:T(8,128)(2,1)} %get-tuple-element.88, bf16[512,4096]{1,0:T(8,128)(2,1)} %get-tuple-element.87), kind=kOutput, calls=%fused_computation.27 | convolution fusion | flops 17197694976 | bytes 44040192 | tf_op jit(solution)/shard_map/dot_general | solution.py:31
  857.7 38.8 %reduce-scatter.15.cloned.1.call-done = bf16[128,2048]{1,0:T(8,128)(2,1)} async-done(((bf16[512,2048]{1,0:T(8,128)(2,1)}), bf16[128,2048]{1,0:T(8,128)(2,1)}) %reduce-scatter.15.cloned.1.call-update) | async-done | bytes 524304 | tf_op jit(solution)/shard_map/reduce_scatter | solution.py:177
  966.1 34.3 %all-reduce.19.cloned.1.call-done = (bf16[512,256]{1,0:T(8,128)(2,1)}, bf16[512,256]{1,0:T(8,128)(2,1)}, bf16[512,256]{0,1:T(8,128)(2,1)}) async-done(((bf16[512,256]{1,0:T(8,128)(2,1)}, bf16[512,256]{1,0:T(8,128)(2,1)}, bf16[512,256]{0,1:T(8,128)(2,1)}), (bf16[512,256]{1,0:T(8,128)(2,1)}, bf16[512,256]{1,0:T(8,128)(2,1)}, bf16[512,256]{0,1:T(8,128)(2,1)})) %all-reduce.19.cloned.1.call-update) | async-done | bytes 786448 | tf_op jit(solution)/shard_map/psum | solution.py:188
  1045.8 25.2 %convolution_convert_fusion = bf16[2048,8192]{1,0:T(8,128)(2,1)} fusion(bf16[512,2048]{1,0:T(8,128)(2,1)} %all-gather.22.cloned.1.call-done, bf16[512,4096]{1,0:T(8,128)(2,1)} %get-tuple-element.88, bf16[512,4096]{1,0:T(8,128)(2,1)} %get-tuple-element.87), kind=kOutput, calls=%fused_computation.5 | convolution fusion | flops 17213423616 | bytes 44040192 | tf_op jit(solution)/shard_map/dot_general | solution.py:25
  1071.0 54.5 %convert_element_type.265 = bf16[2048,2,4096]{2,1,0:T(2,128)(2,1)} reshape(bf16[2048,8192]{1,0:T(8,128)(2,1)} %convolution_convert_fusion) | data formatting | bytes 67108864 | tf_op jit(solution)/shard_map/convert_element_type | solution.py:446
  1185.2 24.4 %reduce-scatter.25.cloned.1.call-done = bf16[512,256]{1,0:T(8,128)(2,1)} async-done(((bf16[512,2048]{1,0:T(8,128)(2,1)}), bf16[512,256]{1,0:T(8,128)(2,1)}) %reduce-scatter.25.cloned.1.call-update) | async-done | bytes 262160 | tf_op jit(solution)/shard_map/reduce_scatter | solution.py:454
  1211.4 39.1 %reduce-scatter.19.cloned.1.call-done = bf16[256,512]{1,0:T(8,128)(2,1)} async-done(((bf16[2048,512]{1,0:T(8,128)(2,1)}), bf16[256,512]{1,0:T(8,128)(2,1)}) %reduce-scatter.19.cloned.1.call-update) | async-done | bytes 262160 | tf_op jit(solution)/shard_map/reduce_scatter | solution.py:436
  1252.2 39.3 %all-reduce.1 = (f32[2048]{0:T(1024)}, f32[2048]{0:T(1024)}) all-reduce(f32[2048]{0:T(1024)S(1)} %get-tuple-element.73, f32[2048]{0:T(1024)S(1)} %get-tuple-element.71), channel_id=1, replica_groups=mesh['row'=4,'col'=8] {'row','col'}, use_global_device_ids=true, to_apply=%region_20.21 | all-reduce | flops 4096 | bytes 32768 | tf_op jit(solution)/shard_map/psum | solution.py:476
  1291.5 113.4 %all-reduce.17.cloned.1.call-done = (bf16[256,512]{1,0:T(8,128)(2,1)}, bf16[256,512]{1,0:T(8,128)(2,1)}, bf16[512,256]{1,0:T(8,128)(2,1)}, bf16[256,2,4096]{2,1,0:T(2,128)(2,1)}, bf16[4096,256]{1,0:T(8,128)(2,1)}) async-done(((bf16[256,512]{1,0:T(8,128)(2,1)}, bf16[256,512]{1,0:T(8,128)(2,1)}, bf16[512,256]{1,0:T(8,128)(2,1)}, bf16[256,2,4096]{2,1,0:T(2,128)(2,1)}, bf16[4096,256]{1,0:T(8,128)(2,1)}), ...) | async-done | bytes 7077904 | tf_op jit(solution)/shard_map/psum | solution.py:468
  1424.0 19.2 reduce-scatter.21.cloned.1.call-done
  1446.7 646.0 %all-reduce.13.cloned.1.call-done = bf16[2048,2,4096]{2,1,0:T(2,128)(2,1)} async-done(((bf16[2048,2,4096]{2,1,0:T(2,128)(2,1)}), bf16[2048,2,4096]{2,1,0:T(2,128)(2,1)}) %all-reduce.13.cloned.1.call-update) | async-done | bytes 33554448
  2102.7 160.4 %reduce-scatter.29.cloned.1.call-done = bf16[4096,256]{1,0:T(8,128)(2,1)} async-done(((bf16[4096,2048]{1,0:T(8,128)(2,1)}), bf16[4096,256]{1,0:T(8,128)(2,1)}) %reduce-scatter.29.cloned.1.call-update) | async-done | bytes 2097168 | tf_op jit(solution)/shard_map/reduce_scatter | solution.py:457
  2267.0 142.8 %all-reduce.15.cloned.1.call-done = (f32[256,2048]{1,0:T(8,128)}, f32[256,2048]{1,0:T(8,128)}) async-done(((f32[256,2048]{1,0:T(8,128)}, f32[256,2048]{1,0:T(8,128)}), (f32[256,2048]{1,0:T(8,128)}, f32[256,2048]{1,0:T(8,128)})) %all-reduce.15.cloned.1.call-update) | async-done | bytes 4194320 | tf_op jit(solution)/shard_map/psum | solution.py:476
  (368 shorter events, 369.4 us)
Async XLA Ops:
  45.1 95.4 %all-gather.14.cloned.1.call-start = ((), (), s32[]{:S(2)}) async-start(), calls=%async_computation.15 | async-start | bytes 2359296 | tf_op jit(solution)/shard_map/all_gather | solution.py:261
  45.7 126.3 %all-gather.20.cloned.1.call-start = ((), (), s32[]{:S(2)}) async-start(), calls=%async_computation.18 | async-start | bytes 2359296 | tf_op jit(solution)/shard_map/all_gather | solution.py:265
  46.3 187.4 %reduce-scatter.11.cloned.1.call-start = ((), (), s32[]{:S(2)}) async-start(), calls=%async_computation.19 | async-start | bytes 5898240 | tf_op jit(solution)/shard_map/reduce_scatter | solution.py:155
  177.5 113.8 %all-gather.26.cloned.1.call-start = ((), (), s32[]{:S(2)}) async-start(), calls=%async_computation.22 | async-start | bytes 1179648 | tf_op jit(solution)/shard_map/all_gather | solution.py:264
  178.3 126.2 %all-gather.22.cloned.1.call-start = ((), (), s32[]{:S(2)}) async-start(), calls=%async_computation.20 | async-start | bytes 2621440 | tf_op jit(solution)/shard_map/all_gather | solution.py:145
  237.7 357.1 %all-gather.24.cloned.1.call-start = ((), (), s32[]{:S(2)}) async-start(), calls=%async_computation.21 | async-start | bytes 37748736 | tf_op jit(solution)/shard_map/all_gather | solution.py:263
  238.5 428.7 %all-gather.30.cloned.1.call-start = ((), (), s32[]{:S(2)}) async-start(), calls=%async_computation.25 | async-start | bytes 2621440 | tf_op jit(solution)/shard_map/all_gather | solution.py:167
  266.2 517.1 %all-gather.28.cloned.1.call-start = ((), (), s32[]{:S(2)}) async-start(), calls=%async_computation.23 | async-start | bytes 18874368 | tf_op jit(solution)/shard_map/all_gather | solution.py:266
  266.9 590.8 %all-reduce.11.cloned.1.call-start = ((), (), s32[]{:S(2)}) async-start(), calls=%async_computation.27 | async-start | bytes 524288 | tf_op jit(solution)/shard_map/psum | solution.py:188
  816.3 80.1 %reduce-scatter.15.cloned.1.call-start = ((), (), s32[]{:S(2)}) async-start(), calls=%async_computation.26 | async-start | bytes 2621440 | tf_op jit(solution)/shard_map/reduce_scatter | solution.py:177
  841.3 96.4 %all-gather.32.cloned.1.call-start = ((), (), s32[]{:S(2)}) async-start(), calls=%async_computation.28 | async-start | bytes 2621440 | tf_op jit(solution)/shard_map/all_gather | solution.py:167
  901.7 98.7 %all-reduce.19.cloned.1.call-start = ((), (), s32[]{:S(2)}) async-start(), calls=%async_computation.39 | async-start | bytes 1572864 | tf_op jit(solution)/shard_map/psum | solution.py:188
  951.4 196.4 %reduce-scatter.13.cloned.1.call-start = ((), (), s32[]{:S(2)}) async-start(), calls=%async_computation.24 | async-start | bytes 5898240 | tf_op jit(solution)/shard_map/reduce_scatter | solution.py:155
  957.7 200.6 %reduce-scatter.17.cloned.1.call-start = ((), (), s32[]{:S(2)}) async-start(), calls=%async_computation.29 | async-start | bytes 2621440 | tf_op jit(solution)/shard_map/reduce_scatter | solution.py:177
  962.6 217.6 %reduce-scatter.27.cloned.1.call-start = ((), (), s32[]{:S(2)}) async-start(), calls=%async_computation.34 | async-start | bytes 1179648 | tf_op jit(solution)/shard_map/reduce_scatter | solution.py:451
  966.0 215.8 %reduce-scatter.23.cloned.1.call-start = ((), (), s32[]{:S(2)}) async-start(), calls=%async_computation.32 | async-start | bytes 1179648 | tf_op jit(solution)/shard_map/reduce_scatter | solution.py:442
  1008.5 201.1 %reduce-scatter.25.cloned.1.call-start = ((), (), s32[]{:S(2)}) async-start(), calls=%async_computation.33 | async-start | bytes 2359296 | tf_op jit(solution)/shard_map/reduce_scatter | solution.py:454
  1012.9 237.5 %reduce-scatter.19.cloned.1.call-start = ((), (), s32[]{:S(2)}) async-start(), calls=%async_computation.30 | async-start | bytes 2359296 | tf_op jit(solution)/shard_map/reduce_scatter | solution.py:436
  1017.3 387.6 %all-reduce.17.cloned.1.call-start = ((), (), s32[]{:S(2)}) async-start(), calls=%async_computation.38 | async-start | bytes 14155776 | tf_op jit(solution)/shard_map/psum | solution.py:468
  1041.3 401.9 %reduce-scatter.21.cloned.1.call-start = ((), (), s32[]{:S(2)}) async-start(), calls=%async_computation.31 | async-start | bytes 2359296 | tf_op jit(solution)/shard_map/reduce_scatter | solution.py:439
  1045.8 1047.0 %all-reduce.13.cloned.1.call-start = ((), (), s32[]{:S(2)}) async-start(), calls=%async_computation.36 | async-start | bytes 67108864
  1125.6 1137.6 %reduce-scatter.29.cloned.1.call-start = ((), (), s32[]{:S(2)}) async-start(), calls=%async_computation.35 | async-start | bytes 18874368 | tf_op jit(solution)/shard_map/reduce_scatter | solution.py:457
  1155.1 1254.7 %all-reduce.15.cloned.1.call-start = ((), (), s32[]{:S(2)}) async-start(), calls=%async_computation.37 | async-start | bytes 8388608 | tf_op jit(solution)/shard_map/psum | solution.py:476
  1172.7 272.3 %all-to-all-start.3 = ((bf16[8,16,2048]{2,1,0:T(8,128)(2,1)}), bf16[8,16,2048]{2,1,0:T(8,128)(2,1)S(1)}, u32[]{:S(2)}, u32[]{:S(2)}) async-start(bf16[8,16,2048]{2,1,0:T(8,128)(2,1)} %bitcast.202), calls=%async_computation.7 | async-start | bytes 1048576 | tf_op jit(solution)/shard_map/all_to_all | solution.py:488
  (94 other events, 2401.3 us)
Sparse Core Ops, SparseCore 0:
  9.6 33.5 all-gather.15
  45.6 34.0 all-gather.11
  81.3 29.1 all-gather.17
  142.0 29.9 all-gather.19
  177.7 55.9 reduce-scatter.10
  266.2 38.2 all-gather.21
  306.1 288.5 all-gather.23
  596.5 33.3 all-gather.29
  631.5 151.7 all-gather.27
  816.4 41.2 all-reduce.10
  861.2 35.1 reduce-scatter.14
  901.8 35.8 all-gather.31
  951.6 48.7 all-reduce.18
  1003.8 56.9 reduce-scatter.12
  1064.2 35.1 reduce-scatter.16
  1101.6 32.5 reduce-scatter.26
  1136.5 32.5 reduce-scatter.22
  1171.2 38.3 reduce-scatter.24
  1212.5 37.9 reduce-scatter.18
  1254.4 150.5 all-reduce.16
  1407.2 35.9 reduce-scatter.20
  1445.6 647.1 all-reduce.12
  2095.1 167.9 reduce-scatter.28
  2268.7 141.0 all-reduce.14
  (2 shorter events, 56.9 us)
where the time goes:
time: 2430 us; the launch traced here: 2420 us
  waiting for transfers between devices  1850 us (76%)
  matrix products  254 us (10%)
  local copies, waits for them, and re-layouts  131 us (5%)
  blocking collectives  86.2 us (4%)
  other arithmetic  65.2 us (3%)
    unnamed x27, waiting for transfers between devices  651 us
    all_gather x1, waiting for transfers between devices, per_device(): lax.all_gather(gate_up_weight, 'col', axis=0, tiled=True)  288 us
    reduce_scatter x1, waiting for transfers between devices, per_device(): lax.psum_scatter(grad_shrink.astype(jnp.bfloat16), 'col', scatter_dimensi...  160 us
    psum x1, waiting for transfers between devices, per_device(): lax.psum((output_second_gradient, narrow_second_gradient, grad_attn_gain,...  143 us
    all_gather x1, waiting for transfers between devices, per_device(): lax.all_gather(down_projection_weight, 'col', axis=1, tiled=True)  116 us
    psum x1, waiting for transfers between devices, per_device(): lax.psum(query_second_gradient.astype(jnp.bfloat16), 'col')  113 us
    dot_general x14, matrix products, inner_column_count(): lax.dot_general(left_op, right_op, (((1,), (1,)), ((), ())), preferred_el...  83.2 us
    dot_general x14, matrix products, matrix_product(): return jnp.dot(left_op, right_op, preferred_element_type=jnp.float32)  82.7 us
  transfers between devices with their start and end apart: 29, of which 21 were waited for; matrix products, arithmetic and copies ran while one was open for 16% of the time, Pallas kernels for 0%

commit v1 on v0

v1 whole, which is shorter than its diff:
```python
import math

import jax
import jax.numpy as jnp
from jax import lax
from jax.experimental import pallas as pl
from jax.experimental.pallas import tpu as pltpu
from jax.sharding import PartitionSpec as P


EPSILON = 1e-06
MASKED = -1e30
CORES = 2


def matrix_product(left_op, right_op):
    return jnp.dot(left_op, right_op, preferred_element_type=jnp.float32)


def inner_row_count(left_op, right_op):
    return lax.dot_general(
        left_op, right_op, (((0,), (0,)), ((), ())), preferred_element_type=jnp.float32
    )


def inner_column_count(left_op, right_op):
    return lax.dot_general(
        left_op, right_op, (((1,), (1,)), ((), ())), preferred_element_type=jnp.float32
    )


def normalize(values, norm_gain):
    inverse = lax.rsqrt(jnp.mean(values * values, axis=1, keepdims=True) + EPSILON)
    return values * inverse * norm_gain


def rotary_tables(positions, head_dim):
    half_dim = head_dim // 2
    inverse_freq = jnp.exp(
        jnp.arange(half_dim, dtype=jnp.float32) * (-2.0 * math.log(10000.0) / head_dim)
    )
    angles = positions.astype(jnp.float32)[:, None] * inverse_freq[None, :]
    return (jnp.cos(angles), jnp.sin(angles))


def rotate(values, cosine, sine_table):
    half_dim = values.shape[-1] // 2
    first_half = values[..., :half_dim]
    second_half = values[..., half_dim:]
    return jnp.concatenate(
        [
            first_half * cosine - second_half * sine_table,
            second_half * cosine + first_half * sine_table,
        ],
        axis=-1,
    )


def group_layout(lengths, places):
    seq_ends = jnp.cumsum(lengths, axis=-1)
    starts = seq_ends - lengths
    segment = jnp.sum((places[:, None] >= seq_ends[None, :]).astype(jnp.int32), axis=-1)
    chosen = segment[:, None] == jnp.arange(lengths.shape[0], dtype=jnp.int32)[None, :]
    offsets = jnp.sum(jnp.where(chosen, starts[None, :], 0), axis=-1)
    return (segment, places - offsets)


def low(values):
    return values.astype(jnp.bfloat16)


def wide(values):
    return values.astype(jnp.float32)


def swap_row(values, step):
    return lax.ppermute(values, "row", [(s, s ^ step) for s in range(lax.axis_size("row"))])


def swap_z(values, step):
    return lax.ppermute(
        values, "col", [(s, s ^ (CORES * step)) for s in range(lax.axis_size("col"))]
    )


def swap_core(values):
    return lax.ppermute(values, "col", [(s, s ^ 1) for s in range(lax.axis_size("col"))])


def spread_row(values):
    return [values] + [swap_row(values, d) for d in range(1, lax.axis_size("row"))]


def spread_wide(values):
    if lax.axis_size("row") != 4:
        return spread_row(values)
    size = values.shape[0] // 2
    first = swap_row(values, 1)
    second = swap_row(values, 2)
    corner = jnp.concatenate([swap_row(first[:size], 2), swap_row(second[size:], 1)])
    return [values, first, second, corner]


def absolute(blocks, index):
    bit = 1
    while bit < len(blocks):
        taken = (index & bit) != 0
        blocks = [jnp.where(taken, blocks[i ^ bit], blocks[i]) for i in range(len(blocks))]
        bit *= 2
    return blocks


def spread_z(values):
    found = {0: values}
    step = lax.axis_size("col") // CORES // 2
    while step > 0:
        for d, block in list(found.items()):
            found[d ^ step] = swap_z(block, step)
        step //= 2
    return [found[d] for d in range(len(found))]


def tree_sum(parts):
    while len(parts) > 1:
        parts = [parts[i] + parts[i + 1] for i in range(0, len(parts), 2)]
    return parts[0]


def scatter_row(blocks):
    return tree_sum(
        [wide(blocks[0])]
        + [wide(swap_row(low(b), d)) for d, b in enumerate(blocks) if d > 0]
    )


def scatter_z(blocks):
    return tree_sum(
        [wide(blocks[0])]
        + [wide(swap_z(low(b), d)) for d, b in enumerate(blocks) if d > 0]
    )


def row_blocks(values, count):
    size = values.shape[0] // count
    return [values[i * size : (i + 1) * size] for i in range(count)]


def piece(values, index, count, axis):
    size = values.shape[axis] // count
    return lax.dynamic_slice_in_dim(values, index * size, size, axis)


def total_all(values):
    values = tree_sum(spread_row(values))
    values = tree_sum(spread_z(values))
    return values + swap_core(values)


def gelu_parts(gate):
    scale = math.sqrt(2.0 / math.pi)
    cube = 0.044715 * gate * gate * gate
    tanh = jnp.tanh(scale * (gate + cube))
    half = 0.5 * (1.0 + tanh)
    slope = half + 0.5 * gate * (1.0 - tanh * tanh) * scale * (1.0 + 3 * 0.044715 * gate * gate)
    return (gate * half, slope)


def norm_back(values, norm_gain, incoming):
    inverse = lax.rsqrt(jnp.mean(values * values, axis=1, keepdims=True) + EPSILON)
    scaled = incoming * norm_gain
    mean_product = jnp.mean(scaled * values, axis=1, keepdims=True)
    grad = inverse * scaled - values * (inverse * inverse * inverse) * mean_product
    return (grad, jnp.sum(incoming * values * inverse, axis=0))


def assemble(blocks, indices, axis, splits=None):
    height, breadth = blocks[0].shape
    splits = [breadth] if splits is None else splits
    count = len(blocks)

    def body(index_ref, *refs):
        block_refs, out_refs = refs[:count], refs[count:]
        for i in range(count):

            @pl.when(pl.program_id(0) == i)
            def _(i=i):
                at = 0
                for size, out_ref in zip(splits, out_refs):
                    out_ref[...] = block_refs[i][:, at : at + size]
                    at += size

    if axis == 0:
        shapes = [(height * count, size) for size in splits]
        out_specs = [pl.BlockSpec((height, size), lambda i, o: (o[i], 0)) for size in splits]
    else:
        shapes = [(height, breadth * count)]
        out_specs = [pl.BlockSpec((height, breadth), lambda i, o: (0, o[i]))]
    results = pl.pallas_call(
        body,
        grid_spec=pltpu.PrefetchScalarGridSpec(
            num_scalar_prefetch=1,
            grid=(count,),
            in_specs=[pl.BlockSpec((height, breadth), lambda i, o: (0, 0))] * count,
            out_specs=out_specs,
        ),
        out_shape=[jax.ShapeDtypeStruct(shape, blocks[0].dtype) for shape in shapes],
        name="assemble",
    )(jnp.stack(indices).astype(jnp.int32), *blocks)
    return results if len(results) > 1 else results[0]


def pack_units(order, flat, tall, half):
    rows = flat.shape[0]
    count = flat.shape[1] // (2 * half)

    def body(order_ref, gate_ref, up_ref, tall_ref, out_ref):
        out_ref[0] = gate_ref[...]
        out_ref[1] = up_ref[...]
        out_ref[2] = low(wide(tall_ref[...]).T)

    return pl.pallas_call(
        body,
        grid_spec=pltpu.PrefetchScalarGridSpec(
            num_scalar_prefetch=1,
            grid=(order.shape[0],),
            in_specs=[
                pl.BlockSpec((rows, half), lambda i, o: (0, o[i])),
                pl.BlockSpec((rows, half), lambda i, o: (0, count + o[i])),
                pl.BlockSpec((half, rows), lambda i, o: (o[i], 0)),
            ],
            out_specs=pl.BlockSpec((None, 3, rows, half), lambda i, o: (i, 0, 0, 0)),
        ),
        out_shape=jax.ShapeDtypeStruct((order.shape[0], 3, rows, half), jnp.bfloat16),
        name="pack_units",
    )(order, flat, flat, tall)


def join_units(order, blocks, rank_block):
    _, rows, half = blocks[0].shape
    rank = rank_block.shape[1]
    steps = len(blocks)
    more = rank // rows

    def body(order_ref, *refs):
        block_refs, rank_ref, out_refs = refs[:steps], refs[steps], refs[steps + 1 :]
        for i in range(steps):

            @pl.when(pl.program_id(0) == i)
            def _(i=i):
                for j in range(3):
                    out_refs[j][...] = block_refs[i][j]

        for i in range(more):

            @pl.when(pl.program_id(0) == steps + i)
            def _(i=i):
                for j in range(3):
                    out_refs[j][...] = rank_ref[j, i * rows : (i + 1) * rows, :]

    extended = rows * steps + rank
    return pl.pallas_call(
        body,
        grid_spec=pltpu.PrefetchScalarGridSpec(
            num_scalar_prefetch=1,
            grid=(steps + more,),
            in_specs=[pl.BlockSpec((3, rows, half), lambda i, o: (0, 0, 0))] * steps
            + [pl.BlockSpec((3, rank, half), lambda i, o: (0, 0, 0))],
            out_specs=[pl.BlockSpec((rows, half), lambda i, o: (o[i], 0))] * 3,
        ),
        out_shape=[jax.ShapeDtypeStruct((extended, half), jnp.bfloat16)] * 3,
        compiler_params=pltpu.CompilerParams(vmem_limit_bytes=56 * 1024 * 1024),
        name="join_units",
    )(order, *blocks, rank_block)


def pick_columns(places, grads, rows):
    half = grads[0].shape[1]
    count = places.shape[0]

    def body(place_ref, *refs):
        for j, grad_ref in enumerate(refs[:-1]):
            refs[-1][j] = grad_ref[...]

    return pl.pallas_call(
        body,
        grid_spec=pltpu.PrefetchScalarGridSpec(
            num_scalar_prefetch=1,
            grid=(count,),
            in_specs=[pl.BlockSpec((rows, half), lambda i, o: (o[i], 0))] * len(grads),
            out_specs=pl.BlockSpec((None, len(grads), rows, half), lambda i, o: (i, 0, 0, 0)),
        ),
        out_shape=jax.ShapeDtypeStruct((count, len(grads), rows, half), jnp.bfloat16),
        name="pick_columns",
    )(places, *grads)


def merge_columns(places, grads, arrived):
    count, parts, rows, half = arrived.shape

    def body(place_ref, *refs):
        arrived_ref, out_ref = refs[-2:]
        for j, grad_ref in enumerate(refs[:-2]):
            out_ref[j] = low(wide(grad_ref[...]) + wide(arrived_ref[j ^ 1]))

    whole = pl.BlockSpec((None, parts, rows, half), lambda i, o: (i, 0, 0, 0))
    return pl.pallas_call(
        body,
        grid_spec=pltpu.PrefetchScalarGridSpec(
            num_scalar_prefetch=1,
            grid=(count,),
            in_specs=[pl.BlockSpec((rows, half), lambda i, o: (o[i], 0))] * parts + [whole],
            out_specs=whole,
        ),
        out_shape=jax.ShapeDtypeStruct(arrived.shape, jnp.bfloat16),
        name="merge_columns",
    )(places, *grads, arrived)


def unpack_units(order, parts, specs, rows, half, count):
    def body(order_ref, gate_ref, up_ref, tall_ref, pair_out, tall_out):
        pair_out[:, 0, :] = wide(gate_ref[...])
        pair_out[:, 1, :] = wide(up_ref[...])
        tall_out[...] = wide(tall_ref[...]).T

    return pl.pallas_call(
        body,
        grid_spec=pltpu.PrefetchScalarGridSpec(
            num_scalar_prefetch=1,
            grid=(count,),
            in_specs=specs,
            out_specs=[
                pl.BlockSpec((rows, 2, half), lambda i, o: (0, 0, o[i])),
                pl.BlockSpec((half, rows), lambda i, o: (o[i], 0)),
            ],
        ),
        out_shape=[
            jax.ShapeDtypeStruct((rows, 2, half * count), jnp.float32),
            jax.ShapeDtypeStruct((half * count, rows), jnp.float32),
        ],
        name="unpack_units",
    )(order, *parts)


def chunk_inner(values, gradient, own, other, chunk, kept, total):
    size, extended = values.shape
    half = own[0].shape[1]
    tile = min(256, half)
    tiles = half // tile
    copying = total > size

    def body(*refs):
        x_ref, g_ref = refs[:2]
        own_refs, other_refs = refs[2:5], refs[5:8]
        refs = refs[8 + (8 if kept is not None else 0) :]
        act_refs, gate_refs, up_refs = refs[0:2], refs[2:4], refs[4:6]
        step = pl.program_id(0)

        def part(weights, h):
            gate = jnp.dot(x_ref[...], weights[0][...], preferred_element_type=jnp.float32)
            up = jnp.dot(x_ref[...], weights[1][...], preferred_element_type=jnp.float32)
            incoming = jnp.dot(g_ref[...], weights[2][...], preferred_element_type=jnp.float32)
            value, slope = gelu_parts(gate)
            act_refs[h][...] = low(value * up)
            gate_refs[h][...] = low(incoming * up * slope)
            up_refs[h][...] = low(incoming * value)

        @pl.when(step < tiles)
        def _():
            part(own_refs, 0)

        @pl.when(step >= tiles)
        def _():
            part(other_refs, 1)

        if copying:

            @pl.when(step == 0)
            def _():
                refs[6][...] = x_ref[...]
                refs[7][...] = g_ref[...]

    def own_map(t):
        return jnp.minimum(t, tiles - 1)

    def other_map(t):
        return jnp.maximum(t - tiles, 0)

    row_spec = pl.BlockSpec((size, extended), lambda t: (0, 0))
    in_specs = [row_spec, row_spec]
    in_specs += [pl.BlockSpec((extended, tile), lambda t: (0, own_map(t)))] * 3
    in_specs += [pl.BlockSpec((extended, tile), lambda t: (0, other_map(t)))] * 3
    operands = [values, gradient, *own, *other]
    aliases = {}
    if kept is not None:
        in_specs += [pl.BlockSpec(memory_space=pl.ANY)] * 8
        aliases = {8 + i: i for i in range(8)}
        operands += list(kept)
    at = chunk if copying else 0
    out_specs = [
        pl.BlockSpec((size, tile), lambda t: (at, own_map(t))),
        pl.BlockSpec((size, tile), lambda t: (at, other_map(t))),
    ] * 3
    out_shape = [jax.ShapeDtypeStruct((total, half), jnp.bfloat16)] * 6
    if copying:
        out_specs += [pl.BlockSpec((size, extended), lambda t: (at, 0))] * 2
        out_shape += [jax.ShapeDtypeStruct((total, extended), jnp.bfloat16)] * 2
    return pl.pallas_call(
        body,
        grid=(2 * tiles,),
        in_specs=in_specs,
        out_specs=out_specs,
        out_shape=out_shape,
        input_output_aliases=aliases,
        compiler_params=pltpu.CompilerParams(vmem_limit_bytes=56 * 1024 * 1024),
        name="chunk_inner",
    )(*operands)


def chunk_outer(kept, own, other, chunk, size):
    half = own[0].shape[1]
    extended = own[0].shape[0]
    tile = 256

    def body(*refs):
        acts, gates, ups = refs[0:2], refs[2:4], refs[4:6]
        weights = (refs[6:9], refs[9:12])
        result_ref, middle_ref = refs[12:]

        def back(left, right):
            return lax.dot_general(
                left[...], right[...], (((1,), (1,)), ((), ())), preferred_element_type=jnp.float32
            )

        result_ref[...] = low(back(acts[0], weights[0][2]) + back(acts[1], weights[1][2]))
        middle_ref[...] = low(
            back(gates[0], weights[0][0])
            + back(gates[1], weights[1][0])
            + back(ups[0], weights[0][1])
            + back(ups[1], weights[1][1])
        )

    return pl.pallas_call(
        body,
        grid=(extended // tile,),
        in_specs=[pl.BlockSpec((size, half), lambda n: (chunk, 0))] * 6
        + [pl.BlockSpec((tile, half), lambda n: (n, 0))] * 6,
        out_specs=[pl.BlockSpec((size, tile), lambda n: (0, n))] * 2,
        out_shape=[jax.ShapeDtypeStruct((size, extended), jnp.bfloat16)] * 2,
        compiler_params=pltpu.CompilerParams(vmem_limit_bytes=56 * 1024 * 1024),
        name="chunk_outer",
    )(*kept[:6], *own, *other)


def per_device(
    tokens,
    cotangent,
    permutation,
    lengths,
    attention_gain,
    query_projection_weight,
    key_value_weight,
    projection_adapter_first,
    query_adapter_second,
    key_value_second,
    output_projection_weight,
    output_adapter_first,
    output_adapter_second,
    hidden_gain,
    gate_up_weight,
    widen_adapter_first,
    widen_adapter_second,
    down_projection_weight,
    narrow_adapter_first,
    narrow_adapter_second,
):
    token_count = tokens.shape[0]
    width = tokens.shape[1]
    rows = lax.axis_size("row")
    cols = lax.axis_size("col")
    depth = cols // CORES
    row = lax.axis_index("row")
    col = lax.axis_index("col")
    layer = col // CORES
    core = col % CORES
    group_size = token_count * rows
    head_dim = key_value_weight.shape[1] // 2
    rank = projection_adapter_first.shape[1]
    slice_width = width // cols
    share = token_count // cols
    half = gate_up_weight.shape[2] // cols

    def by_column(blocks):
        others = [swap_core(b) for b in blocks]
        placed = []
        for d in range(depth):
            placed.append((blocks[d], (layer ^ d) * CORES + core))
            placed.append((others[d], (layer ^ d) * CORES + 1 - core))
        return placed

    def deal(values):
        return lax.all_to_all(
            values.reshape(cols, share, width), "col", split_axis=0, concat_axis=0, tiled=True
        ).reshape(token_count, width)

    def reduce_col(stacked):
        own = lax.dynamic_index_in_dim(stacked, core, 1, keepdims=False)
        other = lax.dynamic_index_in_dim(stacked, 1 - core, 1, keepdims=False)
        summed = low(wide(own) + wide(swap_core(other)))
        blocks = [
            lax.dynamic_index_in_dim(summed, layer ^ d, 0, keepdims=False) for d in range(depth)
        ]
        return scatter_z(blocks)

    targets = jnp.arange(cols, dtype=jnp.int32)[:, None]
    slot_ids = jnp.arange(share, dtype=jnp.int32)[None, :]
    packed = (targets * rows + row) * token_count + col * share + slot_ids
    sources = jnp.take(permutation, packed.reshape(-1)) - (row * cols + col) * token_count
    residual_stream = wide(deal(tokens[sources]))
    output_gradient_rows = deal(cotangent[sources])

    places = jnp.concatenate(
        [(row ^ d) * token_count + jnp.arange(token_count, dtype=jnp.int32) for d in range(rows)]
    )
    segment, positions = group_layout(lengths[0], places)
    cosine, sine_table = rotary_tables(positions, head_dim)
    allowed = (segment[:, None] == segment[None, :]) & (places[None, :] <= places[:, None])

    query_width = query_projection_weight.shape[1]
    shared_weights = jnp.concatenate(
        [key_value_weight, projection_adapter_first, widen_adapter_first], axis=1
    )
    shared_width = shared_weights.shape[1]
    mine = jnp.concatenate(
        [query_projection_weight, piece(shared_weights, row, rows, 1)], axis=1
    )
    placed = by_column(spread_z(mine))
    query_complete, shared_mine = assemble(
        [p[0] for p in placed],
        [p[1] for p in placed],
        0,
        [query_width, shared_width // rows],
    )
    shared_full = assemble(spread_row(shared_mine), [row ^ d for d in range(rows)], 1)
    key_value_complete = shared_full[:, : 2 * head_dim]
    projection_first_complete = shared_full[:, 2 * head_dim : 2 * head_dim + rank]
    widen_first_complete = shared_full[:, 2 * head_dim + rank :]
    placed = by_column(spread_z(output_projection_weight))
    output_blocks = [p[0] for p in placed]
    output_index = [p[1] for p in placed]
    for i in range(rank // slice_width):
        output_blocks.append(output_adapter_first[:, i * slice_width : (i + 1) * slice_width])
        output_index.append(jnp.int32(cols + i))
    output_extended = assemble(output_blocks, output_index, 1)

    flat_main = lax.optimization_barrier(gate_up_weight.reshape(slice_width, -1))
    flat_rank = lax.optimization_barrier(widen_adapter_second.reshape(rank, -1))

    def relative(step):
        return (col ^ step).astype(jnp.int32)

    own_units = pack_units(
        jnp.stack([relative(CORES * d) for d in range(depth)]),
        flat_main,
        down_projection_weight,
        half,
    )
    partner_units = swap_core(
        pack_units(
            jnp.stack([relative(CORES * d + 1) for d in range(depth)]),
            flat_main,
            down_projection_weight,
            half,
        )
    )
    rank_units = pack_units(relative(0)[None], flat_rank, narrow_adapter_first, half)
    own_units, partner_units, query_complete, output_extended = lax.optimization_barrier(
        (own_units, partner_units, query_complete, output_extended)
    )
    unit_blocks = []
    unit_places = []
    for d in range(depth):
        for k, units in enumerate((own_units, partner_units)):
            unit_blocks.append(swap_z(units[d], d) if d else units[d])
            unit_places.append(relative(CORES * d + k))
    unit_places += [jnp.int32(cols + i) for i in range(rank // slice_width)]
    own_weights = join_units(jnp.stack(unit_places), unit_blocks, rank_units[0])
    other_weights = [swap_core(w) for w in own_weights]

    attn_gain = wide(attention_gain)
    input_rows = jnp.concatenate(spread_row(low(normalize(residual_stream, attn_gain))))
    adapter_projection = low(matrix_product(input_rows, projection_first_complete))
    query_linear = matrix_product(input_rows, query_complete) + matrix_product(
        adapter_projection, query_adapter_second
    )
    key_value_linear = matrix_product(input_rows, key_value_complete) + matrix_product(
        adapter_projection, key_value_second
    )
    heads_local = query_width // head_dim
    query_scale = head_dim ** (-0.5)
    queries = low(
        rotate(
            query_linear.reshape(group_size, heads_local, head_dim),
            cosine[:, None, :],
            sine_table[:, None, :],
        )
        * query_scale
    )
    key_rows = low(rotate(key_value_linear[:, :head_dim], cosine, sine_table))
    value_rows = low(key_value_linear[:, head_dim:])
    head_queries = [queries[:, h, :] for h in range(heads_local)]
    head_probs = []
    mixed_list = []
    for query in head_queries:
        products = inner_column_count(query, key_rows)
        scores = jnp.where(allowed, products, MASKED)
        exponent = jnp.exp(scores - jnp.max(scores, axis=1, keepdims=True))
        probs = exponent / jnp.sum(exponent, axis=1, keepdims=True)
        head_probs.append(probs)
        mixed_list.append(low(matrix_product(low(probs), value_rows)))
    mixed = jnp.concatenate(mixed_list, axis=1)
    attention_sums = low(matrix_product(mixed, output_extended))
    attention_piece = scatter_row(row_blocks(attention_sums, rows))
    adapter_output = low(attention_piece[:, width:])
    hidden_state = (
        residual_stream
        + attention_piece[:, :width]
        + matrix_product(adapter_output, output_adapter_second)
    )
    ffn_gain = wide(hidden_gain)
    middle = low(normalize(hidden_state, ffn_gain))

    def stretch(values, factor_rows):
        return spread_wide(
            jnp.concatenate(spread_z(jnp.concatenate([values, factor_rows], axis=1)))
        )

    gradient_chunks = stretch(
        output_gradient_rows, low(inner_column_count(output_gradient_rows, narrow_adapter_second))
    )
    middle_chunks = stretch(middle, low(matrix_product(middle, widen_first_complete)))
    chunk_size = depth * token_count
    joined = rows <= 4
    total = rows * chunk_size if joined else chunk_size
    kept = None
    kept_list = []
    middle_blocks = []
    result_blocks = []
    for c in range(rows):
        kept = chunk_inner(
            middle_chunks[c],
            gradient_chunks[c],
            own_weights,
            other_weights,
            c,
            kept if joined else None,
            total,
        )
        kept_list.append(kept)
        result_block, middle_block = chunk_outer(
            kept, own_weights, other_weights, c if joined else 0, chunk_size
        )
        result_blocks.append(result_block)
        middle_blocks.append(middle_block)
    if joined:
        pieces = [kept]
    else:
        pieces = [
            [*k, m, g] for k, m, g in zip(kept_list, middle_chunks, gradient_chunks)
        ]
    middle_rows = scatter_row(middle_blocks)
    middle_rows, result_blocks = lax.optimization_barrier((middle_rows, result_blocks))
    middle_piece = scatter_z(row_blocks(middle_rows, depth))

    def core_sum(values):
        return wide(values) + wide(swap_core(values))

    def over_rows(left, right):
        parts = [inner_row_count(p[left], p[right]) for p in pieces]
        return sum(parts[1:], parts[0])

    grads = []
    for left, right in ((6, 2), (6, 4), (7, 0)):
        grads.append(low(over_rows(left, right)))
        grads.append(low(over_rows(left, right + 1)))
    parity = [(layer ^ d) * CORES for d in range(depth)]
    sent = pick_columns(
        jnp.stack([p + 1 - core for p in parity]).astype(jnp.int32), grads, slice_width
    )
    summed = merge_columns(
        jnp.stack([p + core for p in parity]).astype(jnp.int32), grads, swap_core(sent)
    )
    rank_grads = jnp.stack(
        [
            low(wide(grads[2 * j][width:]) + wide(swap_core(grads[2 * j + 1][width:])))
            for j in range(3)
        ]
    )
    summed, rank_grads, result_blocks, middle_piece = lax.optimization_barrier(
        (summed, rank_grads, result_blocks, middle_piece)
    )
    result_piece = scatter_z(row_blocks(scatter_row(result_blocks), depth))
    result_piece, hidden_again = lax.optimization_barrier((result_piece, hidden_state))
    adapter_final = low(result_piece[:, width:])
    block_result_rows = low(
        hidden_again
        + result_piece[:, :width]
        + matrix_product(adapter_final, narrow_adapter_second)
    )
    back_out = deal(block_result_rows)

    unit_stack = jnp.stack([summed[0]] + [swap_z(summed[d], d) for d in range(1, depth)])
    unit_order = jnp.stack([relative(e) for e in range(cols)])
    grad_expand_weight, grad_shrink_weight = unpack_units(
        unit_order,
        [unit_stack] * 3,
        [
            pl.BlockSpec(
                (None, None, slice_width, half),
                lambda i, o, j=j: (i // CORES, CORES * j + i % CORES, 0, 0),
            )
            for j in range(3)
        ],
        slice_width,
        half,
        cols,
    )
    rank_blocks = spread_z(rank_grads)
    rank_blocks = [b for block in rank_blocks for b in (block, swap_core(block))]
    rank_stack = jnp.stack(rank_blocks)
    widen_second_gradient, narrow_first_gradient = unpack_units(
        unit_order,
        [rank_stack] * 3,
        [
            pl.BlockSpec((None, None, rank, half), lambda i, o, j=j: (i, j, 0, 0))
            for j in range(3)
        ],
        rank,
        half,
        cols,
    )

    adapter_middle_gradient = low(middle_piece[:, width:])
    grad_normed_mid = middle_piece[:, :width] + inner_column_count(
        adapter_middle_gradient, widen_first_complete
    )
    grad_hidden_norm, grad_ffn_gain = norm_back(hidden_state, ffn_gain, grad_normed_mid)
    grad_hidden = wide(output_gradient_rows) + grad_hidden_norm
    attention_gradient = low(grad_hidden)

    final_all = jnp.concatenate(
        spread_row(
            jnp.concatenate(
                spread_z(jnp.concatenate([adapter_final, adapter_middle_gradient], axis=1))
            )
        )
    )

    def part_of(values, index, count):
        size = width // count
        return lax.dynamic_slice_in_dim(values, index * size, size, 1)

    def own_chunk(index):
        return final_all[index * chunk_size : (index + 1) * chunk_size] if not joined else final_all

    narrow_second_part = sum(
        inner_row_count(
            own_chunk(i)[:, :rank], part_of(p[7], row * depth + layer, rows * depth)
        )
        for i, p in enumerate(pieces)
    )
    narrow_second_part = low(core_sum(low(narrow_second_part)))
    narrow_second_gradient = wide(
        lax.all_gather(
            piece(narrow_second_part, core, CORES, 1), ("row", "col"), axis=1, tiled=True
        )
    )
    widen_first_part = low(
        sum(
            inner_row_count(
                piece(own_chunk(i)[:, rank:], row, rows, 1), part_of(p[6], layer, depth)
            )
            for i, p in enumerate(pieces)
        )
    )
    widen_first_part = low(
        wide(piece(widen_first_part, core, CORES, 1))
        + wide(swap_core(piece(widen_first_part, 1 - core, CORES, 1)))
    )
    widen_first_gradient = wide(jnp.concatenate(absolute(spread_row(widen_first_part), row))).T

    attention_rows = jnp.concatenate(spread_row(attention_gradient))
    attention_adapter_rows = low(inner_column_count(attention_rows, output_adapter_second))
    adapter_output_rows = jnp.concatenate(spread_row(adapter_output))
    grad_mixed = low(
        inner_column_count(
            jnp.concatenate([attention_rows, attention_adapter_rows], axis=1), output_extended
        )
    )
    output_part = low(inner_row_count(attention_rows, mixed))
    grad_output_weight = reduce_col(output_part.reshape(depth, CORES, slice_width, query_width)).T
    output_first_gradient, output_second_gradient = [
        wide(part)
        for part in lax.psum(
            (
                low(inner_row_count(mixed, attention_adapter_rows)),
                low(inner_row_count(adapter_output_rows, attention_rows)),
            ),
            "col",
        )
    ]

    grad_query_list = []
    grad_key_part = 0.0
    grad_value_part = 0.0
    for h in range(heads_local):
        grad_head = grad_mixed[:, h * head_dim : (h + 1) * head_dim]
        probs = head_probs[h]
        grad_probs = inner_column_count(grad_head, value_rows)
        shared = jnp.sum(probs * grad_probs, axis=1, keepdims=True)
        grad_scores = low(probs * (grad_probs - shared))
        grad_query_head = matrix_product(grad_scores, key_rows)
        grad_query_list.append(
            low(rotate(grad_query_head, cosine, -sine_table) * query_scale)
        )
        grad_key_part = grad_key_part + inner_row_count(grad_scores, head_queries[h])
        grad_value_part = grad_value_part + inner_row_count(low(probs), grad_head)
    query_gradient = jnp.concatenate(grad_query_list, axis=1)
    small_piece = scatter_row(
        row_blocks(
            jnp.concatenate(
                [
                    grad_key_part,
                    grad_value_part,
                    inner_column_count(query_gradient, query_adapter_second),
                ],
                axis=1,
            ),
            rows,
        )
    )
    own_cosine = cosine[:token_count]
    own_sine = sine_table[:token_count]
    own_key_value = low(
        jnp.concatenate(
            [
                rotate(small_piece[:, :head_dim], own_cosine, -own_sine),
                small_piece[:, head_dim : 2 * head_dim],
            ],
            axis=1,
        )
    )
    own_adapter = low(
        small_piece[:, 2 * head_dim :] + inner_column_count(own_key_value, key_value_second)
    )
    input_piece = scatter_row(row_blocks(inner_column_count(query_gradient, query_complete), rows))
    grad_normed_in = (
        input_piece
        + inner_column_count(own_key_value, key_value_complete)
        + inner_column_count(own_adapter, projection_first_complete)
    )
    grad_in_norm, grad_attn_gain = norm_back(residual_stream, attn_gain, grad_normed_in)
    back_grad = deal(low(grad_hidden + grad_in_norm))

    small_rows = jnp.concatenate(
        spread_row(jnp.concatenate([own_key_value, own_adapter], axis=1))
    )
    key_value_mine = piece(small_rows[:, : 2 * head_dim], row, rows, 1)
    adapter_mine = piece(small_rows[:, 2 * head_dim :], row, rows, 1)
    gradient_columns = jnp.concatenate([query_gradient, key_value_mine, adapter_mine], axis=1)
    input_part = low(inner_row_count(input_rows, gradient_columns))
    reduced = reduce_col(input_part.reshape(depth, CORES, slice_width, -1))
    grad_query_weight = reduced[:, :query_width]
    kv_width = 2 * head_dim // rows
    shared_blocks = absolute(spread_row(low(reduced[:, query_width:])), row)
    grad_keyval_weight = wide(jnp.concatenate([b[:, :kv_width] for b in shared_blocks], axis=1))
    projection_first_gradient = wide(
        jnp.concatenate([b[:, kv_width:] for b in shared_blocks], axis=1)
    )
    query_second_gradient, key_value_second_gradient = [
        wide(part)
        for part in lax.psum(
            (
                low(inner_row_count(adapter_projection, query_gradient)),
                low(inner_row_count(adapter_projection, small_rows[:, : 2 * head_dim])),
            ),
            "col",
        )
    ]

    gain_sums = total_all(jnp.stack([grad_attn_gain, grad_ffn_gain]))

    order = jnp.arange(token_count, dtype=jnp.int32)
    inverse = jnp.sum(
        jnp.where(sources[None, :] == order[:, None], order[None, :], 0), axis=1
    )
    return (
        back_out[inverse],
        back_grad[inverse],
        gain_sums[0],
        grad_query_weight,
        grad_keyval_weight,
        projection_first_gradient,
        query_second_gradient,
        key_value_second_gradient,
        grad_output_weight,
        output_first_gradient,
        output_second_gradient,
        gain_sums[1],
        grad_expand_weight,
        widen_first_gradient,
        widen_second_gradient,
        grad_shrink_weight,
        narrow_first_gradient,
        narrow_second_gradient,
    )


def solution(mesh):
    return jax.shard_map(
        per_device,
        mesh=mesh,
        in_specs=(
            P(("row", "col"), None),
            P(("row", "col"), None),
            P(),
            P("col", None),
            P(),
            P("col", "row"),
            P("col", None),
            P("col", None),
            P(None, "row"),
            P(),
            P("row", "col"),
            P("row", None),
            P(),
            P(),
            P("col", None, "row"),
            P("col", None),
            P(None, None, "row"),
            P("row", "col"),
            P("row", None),
            P(),
        ),
        out_specs=(
            P(("row", "col"), None),
            P(("row", "col"), None),
            P(),
            P("col", "row"),
            P("col", None),
            P("col", None),
            P(None, "row"),
            P(),
            P("row", "col"),
            P("row", None),
            P(),
            P(),
            P("col", None, "row"),
            P("col", None),
            P(None, None, "row"),
            P("row", "col"),
            P("row", None),
            P(),
        ),
        check_vma=False,
    )
```

time: 2430 us -> 1400 us (0.58)
  waiting for transfers between devices: 1850 us -> 656 us
  starting transfers between devices: 16.7 us -> 234 us
  Pallas kernels: 0 us -> 197 us
  matrix products: 254 us -> 89.6 us
  blocking collectives: 86.2 us -> 0 us
    ppermute x0 -> x117, waiting for transfers between devices: none -> 654 us  [the longest x42 401 us: swap_z(): lax.ppermute(values, 'col', [(s, s ^ CORES * step) for s in range(lax.axi...]
    unnamed x27 -> x2, waiting for transfers between devices: 651 us -> 0.03 us
    all_gather x11 -> x1, waiting for transfers between devices: 525 us -> 0.01 us  [per_device(): lax.all_gather(piece(narrow_second_part, core, CORES, 1), ('row', 'col'),...]
    reduce_scatter x10 -> x0, waiting for transfers between devices: 337 us -> none  [the longest x1 160 us: per_device(): lax.psum_scatter(grad_shrink.astype(jnp.bfloat16), 'col', scatter_dimensi...]
    psum x4 -> x1, waiting for transfers between devices: 306 us -> 0.01 us  [per_device(): lax.psum((low(inner_row_count(adapter_projection, query_gradient)), low(i...]
    ppermute x0 -> x117, starting transfers between devices: none -> 217 us  [the longest x42 152 us: swap_z(): lax.ppermute(values, 'col', [(s, s ^ CORES * step) for s in range(lax.axi...]
    pallas_call x0 -> x19, Pallas kernels: none -> 197 us  [the longest x4 66 us: chunk_inner(): pl.pallas_call(body, grid=(2 * tiles,), in_specs=in_specs, out_specs=out_...]
    dot_general x14 -> x13, matrix products: 83.2 us -> 14 us  [inner_column_count(): lax.dot_general(left_op, right_op, (((1,), (1,)), ((), ())), preferred_el...]
  transfers between devices with their start and end apart: 29 -> 123, of which waited for: 21 -> 43; matrix products, arithmetic and copies ran while one was open for 16% -> 16% of each run, Pallas kernels for 0% -> 13%
where the time goes in v1:
time: 1400 us; the launch traced here: 1390 us
  waiting for transfers between devices  656 us (47%)
  starting transfers between devices  234 us (17%)
  Pallas kernels  197 us (14%)
  local copies, waits for them, and re-layouts  128 us (9%)
  matrix products  89.6 us (6%)
  other arithmetic  67.1 us (5%)
  between operations  17.8 us (1%)
    ppermute x42, waiting for transfers between devices, swap_z(): lax.ppermute(values, 'col', [(s, s ^ CORES * step) for s in range(lax.axi...  401 us
    ppermute x50, waiting for transfers between devices, swap_row(): lax.ppermute(values, 'row', [(s, s ^ step) for s in range(lax.axis_size('...  251 us
    ppermute x42, starting transfers between devices, swap_z(): lax.ppermute(values, 'col', [(s, s ^ CORES * step) for s in range(lax.axi...  152 us
    pallas_call x4, Pallas kernels, chunk_inner(): pl.pallas_call(body, grid=(2 * tiles,), in_specs=in_specs, out_specs=out_...  66 us
    dot_general x18, matrix products, inner_row_count(): lax.dot_general(left_op, right_op, (((0,), (0,)), ((), ())), preferred_el...  60.7 us
    ppermute x50, starting transfers between devices, swap_row(): lax.ppermute(values, 'row', [(s, s ^ step) for s in range(lax.axis_size('...  60.4 us
    unnamed x286, local copies, waits for them, and re-layouts  58.4 us
    pallas_call x4, Pallas kernels, chunk_outer(): pl.pallas_call(body, grid=(extended // tile,), in_specs=[pl.BlockSpec((si...  57.3 us
  transfers between devices with their start and end apart: 123, of which 43 were waited for; matrix products, arithmetic and copies ran while one was open for 16% of the time, Pallas kernels for 13%

profile of v1, /device:TPU:0, one launch (start us, length us, event | category | flops | bytes accessed | tf_op | source)
XLA Modules:
  0.0 1389.8 jit_solution(6843545107294034881)
XLA Ops:
  26.4 19.4 %collective-permute-done.7.refs_4_ = bf16[256,768]{1,0:T(8,128)(2,1)S(1)} collective-permute-done((bf16[256,768]{1,0:T(8,128)(2,1)S(1)}, bf16[256,768]{1,0:T(8,128)(2,1)S(1)}, u32[]{:S(2)}, u32[]{:S(2)}) %collective-permute-start.7) | collective-permute-done | bytes 393248 | tf_op jit(solution)/shard_map/ppermute | solution.py:81
  122.5 21.0 %collective-permute-done.19.refs_2_ = bf16[2048,256]{1,0:T(8,128)(2,1)} collective-permute-done((bf16[2048,256]{1,0:T(8,128)(2,1)}, bf16[2048,256]{1,0:T(8,128)(2,1)}, u32[]{:S(2)}, u32[]{:S(2)}) %collective-permute-start.19) | collective-permute-done | bytes 1048608 | tf_op jit(solution)/shard_map/ppermute | solution.py:77
  223.9 52.7 %collective-permute-done.25 = bf16[128,2304]{1,0:T(8,128)(2,1)S(1)} collective-permute-done((bf16[128,2304]{1,0:T(8,128)(2,1)S(1)}, bf16[128,2304]{1,0:T(8,128)(2,1)S(1)}, u32[]{:S(2)}, u32[]{:S(2)}) %collective-permute-start.25) | collective-permute-done | bytes 589856 | tf_op jit(solution)/shard_map/ppermute | solution.py:81
  308.3 18.9 %collective-permute-done.40.refs_4_ = bf16[3,256,512]{2,1,0:T(8,128)(2,1)S(1)} collective-permute-done((bf16[3,256,512]{2,1,0:T(8,128)(2,1)S(1)}, bf16[3,256,512]{2,1,0:T(8,128)(2,1)S(1)}, u32[]{:S(2)}, u32[]{:S(2)}) %collective-permute-start.40) | collective-permute-done | bytes 786464 | tf_op jit(solution)/shard_map/ppermute | solution.py:81
  330.0 15.7 %collective-permute-start.41 = (bf16[3,256,512]{2,1,0:T(8,128)(2,1)S(1)}, bf16[3,256,512]{2,1,0:T(8,128)(2,1)S(1)}, u32[]{:S(2)}, u32[]{:S(2)}) collective-permute-start(bf16[3,256,512]{2,1,0:T(8,128)(2,1)S(1)} %get-tuple-element.243), channel_id=1, source_target_pairs={{0,4},{1,5},{2,6},{3,7},{4,0},{5,1},{6,2},{7,3},{8,12},{9,13},{10,... | collective-permute-start | bytes 2359304 | tf_op jit(solution)/shard_map/ppermute | solution.py:81
  345.6 34.6 %collective-permute-done.41.refs_5_ = bf16[3,256,512]{2,1,0:T(8,128)(2,1)S(1)} collective-permute-done((bf16[3,256,512]{2,1,0:T(8,128)(2,1)S(1)}, bf16[3,256,512]{2,1,0:T(8,128)(2,1)S(1)}, u32[]{:S(2)}, u32[]{:S(2)}) %collective-permute-start.41) | collective-permute-done | bytes 786464 | tf_op jit(solution)/shard_map/ppermute | solution.py:81
  420.8 21.2 %collective-permute-done.37 = bf16[256,2304]{1,0:T(8,128)(2,1)S(1)} collective-permute-done((bf16[256,2304]{1,0:T(8,128)(2,1)S(1)}, bf16[256,2304]{1,0:T(8,128)(2,1)S(1)}, u32[]{:S(2)}, u32[]{:S(2)}) %collective-permute-start.37) | collective-permute-done | bytes 1179680 | tf_op jit(solution)/shard_map/ppermute | solution.py:77
  449.0 16.4 %chunk_inner.4 = (bf16[2048,512]{1,0:T(8,128)(2,1)}, bf16[2048,512]{1,0:T(8,128)(2,1)}, bf16[2048,512]{1,0:T(8,128)(2,1)}, bf16[2048,512]{1,0:T(8,128)(2,1)}, bf...) custom-call(bf16[512,2304]{1,0:T(8,128)(2,1)} %pad_maximum_fusion.1., ...), custom_call_target="tpu_custom_call" | custom-call | tf_op jit(solution)/shard_map/chunk_inner/pallas_call | solution.py:407
  465.4 14.2 %chunk_outer.4 = (bf16[512,2304]{1,0:T(8,128)(2,1)}, bf16[512,2304]{1,0:T(8,128)(2,1)}) custom-call(bf16[2048,512]{1,0:T(8,128)(2,1)} %get-tuple-element.94.refs_8_.refs_0_, bf16[2048,512]{1,0:T(8,128)(2,1)} %get-tuple-element.95.refs_9_.refs_1_, bf16[2048,512]{1,0:T(8,128)(2,1)} %get-tuple-element.96.refs_10_.refs_2_, ...), custom_call_target="tpu_custom_call" | custom-call | tf_op jit(solution)/shard_map/chunk_outer/pallas_call | solution.py:442
  479.7 16.5 %chunk_inner.5 = (bf16[2048,512]{1,0:T(8,128)(2,1)}, bf16[2048,512]{1,0:T(8,128)(2,1)}, bf16[2048,512]{1,0:T(8,128)(2,1)}, bf16[2048,512]{1,0:T(8,128)(2,1)}, bf...) custom-call(bf16[512,2304]{1,0:T(8,128)(2,1)} %collective-permute-do, ...), custom_call_target="tpu_custom_call", output_to_operand_aliasing={{0}: (8, {}), {1}: (9, {}), {2}: (10, {}), {3}: (11, {}), {... | custom-call | tf_op jit(solution)/shard_map/chunk_inner/pallas_call | solution.py:407
  510.5 16.5 %chunk_inner.6 = (bf16[2048,512]{1,0:T(8,128)(2,1)}, bf16[2048,512]{1,0:T(8,128)(2,1)}, bf16[2048,512]{1,0:T(8,128)(2,1)}, bf16[2048,512]{1,0:T(8,128)(2,1)}, bf...) custom-call(bf16[512,2304]{1,0:T(8,128)(2,1)} %collective-permute-do, ...), custom_call_target="tpu_custom_call", output_to_operand_aliasing={{0}: (8, {}), {1}: (9, {}), {2}: (10, {}), {3}: (11, {}), {... | custom-call | tf_op jit(solution)/shard_map/chunk_inner/pallas_call | solution.py:407
  527.0 14.7 %chunk_outer.6 = (bf16[512,2304]{1,0:T(8,128)(2,1)}, bf16[512,2304]{1,0:T(8,128)(2,1)}) custom-call(bf16[2048,512]{1,0:T(8,128)(2,1)} %get-tuple-element.110.refs_8_.refs_0_, bf16[2048,512]{1,0:T(8,128)(2,1)} %get-tuple-element.111.refs_9_.refs_1_, bf16[2048,512]{1,0:T(8,128)(2,1)} %get-tuple-element.112.refs_10_.refs_2_, ...), custom_call_target="tpu_custom_call" | custom-call | tf_op jit(solution)/shard_map/chunk_outer/pallas_call | solution.py:442
  544.8 16.5 %chunk_inner.7 = (bf16[2048,512]{1,0:T(8,128)(2,1)}, bf16[2048,512]{1,0:T(8,128)(2,1)}, bf16[2048,512]{1,0:T(8,128)(2,1)}, bf16[2048,512]{1,0:T(8,128)(2,1)}, bf...) custom-call(bf16[512,2304]{1,0:T(8,128)(2,1)} %pad_maximum_fusion.2., ...), custom_call_target="tpu_custom_call", output_to_operand_aliasing={{0}: (8, {}), {1}: (9, {}), {2}: (10, {}), {3}: (11, {}), {... | custom-call | tf_op jit(solution)/shard_map/chunk_inner/pallas_call | solution.py:407
  637.2 27.8 %collective-permute-done.51 = bf16[512,2304]{1,0:T(8,128)(2,1)} collective-permute-done((bf16[512,2304]{1,0:T(8,128)(2,1)}, bf16[512,2304]{1,0:T(8,128)(2,1)}, u32[]{:S(2)}, u32[]{:S(2)}) %collective-permute-start.51) | collective-permute-done | bytes 2359328 | tf_op jit(solution)/shard_map/ppermute | solution.py:77
  665.0 50.3 %collective-permute-done.52 = bf16[512,2304]{1,0:T(8,128)(2,1)} collective-permute-done((bf16[512,2304]{1,0:T(8,128)(2,1)}, bf16[512,2304]{1,0:T(8,128)(2,1)}, u32[]{:S(2)}, u32[]{:S(2)}) %collective-permute-start.52) | collective-permute-done | bytes 2359328 | tf_op jit(solution)/shard_map/ppermute | solution.py:77
  728.1 18.1 %collective-permute-done.54 = bf16[128,2304]{1,0:T(8,128)(2,1)S(1)} collective-permute-done((bf16[128,2304]{1,0:T(8,128)(2,1)S(1)}, bf16[128,2304]{1,0:T(8,128)(2,1)S(1)}, u32[]{:S(2)}, u32[]{:S(2)}) %collective-permute-start.54) | collective-permute-done | bytes 589856 | tf_op jit(solution)/shard_map/ppermute | solution.py:81
  748.2 25.3 %collective-permute-done.55 = bf16[128,2304]{1,0:T(8,128)(2,1)S(1)} collective-permute-done((bf16[128,2304]{1,0:T(8,128)(2,1)S(1)}, bf16[128,2304]{1,0:T(8,128)(2,1)S(1)}, u32[]{:S(2)}, u32[]{:S(2)}) %collective-permute-start.55) | collective-permute-done | bytes 589856 | tf_op jit(solution)/shard_map/ppermute | solution.py:81
  858.1 16.0 %collective-permute-done.81 = bf16[128,768]{0,1:T(8,128)(2,1)S(1)} collective-permute-done((bf16[128,768]{0,1:T(8,128)(2,1)S(1)}, bf16[128,768]{0,1:T(8,128)(2,1)S(1)}, u32[]{:S(2)}, u32[]{:S(2)}) %collective-permute-start.81) | collective-permute-done | bytes 196640 | tf_op jit(solution)/shard_map/ppermute | solution.py:77
  904.2 30.3 %collective-permute-done.73 = f32[2,2048]{1,0:T(2,128)S(1)} collective-permute-done((f32[2,2048]{1,0:T(2,128)S(1)}, f32[2,2048]{1,0:T(2,128)S(1)}, u32[]{:S(2)}, u32[]{:S(2)}) %collective-permute-start.73) | collective-permute-done | bytes 16416 | tf_op jit(solution)/shard_map/ppermute | solution.py:77
  967.3 49.4 %collective-permute-done.112 = bf16[3,256,512]{2,1,0:T(8,128)(2,1)S(1)} collective-permute-done((bf16[3,256,512]{2,1,0:T(8,128)(2,1)}, bf16[3,256,512]{2,1,0:T(8,128)(2,1)S(1)}, u32[]{:S(2)}, u32[]{:S(2)}) %collective-permute-start.112) | collective-permute-done | bytes 786464 | tf_op jit(solution)/shard_map/ppermute | solution.py:81
  1031.3 28.2 %collective-permute-done.98 = bf16[6,256,512]{2,1,0:T(8,128)(2,1)S(1)} collective-permute-done((bf16[6,256,512]{2,1,0:T(8,128)(2,1)}, bf16[6,256,512]{2,1,0:T(8,128)(2,1)S(1)}, u32[]{:S(2)}, u32[]{:S(2)}) %collective-permute-start.98) | collective-permute-done | bytes 1572896 | tf_op jit(solution)/shard_map/ppermute | solution.py:81
  1059.4 83.1 %collective-permute-start.61 = (bf16[128,2304]{1,0:T(8,128)(2,1)S(1)}, bf16[128,2304]{1,0:T(8,128)(2,1)S(1)}, u32[]{:S(2)}, u32[]{:S(2)}) collective-permute-start(bf16[128,2304]{1,0:T(8,128)(2,1)S(1)} %get-tuple-element.254), channel_id=1, source_target_pairs={{0,4},{1,5},{2,6},{3,7},{4,0},{5,1},{6,2},{7,3},{8,12},{9,13},{10,... | collective-permute-start | bytes 1769480 | tf_op jit(solution)/shard_map/ppermute | solution.py:81
  1143.5 56.6 %collective-permute-done.97 = bf16[6,256,512]{2,1,0:T(8,128)(2,1)S(1)} collective-permute-done((bf16[6,256,512]{2,1,0:T(8,128)(2,1)}, bf16[6,256,512]{2,1,0:T(8,128)(2,1)S(1)}, u32[]{:S(2)}, u32[]{:S(2)}) %collective-permute-start.97) | collective-permute-done | bytes 1572896 | tf_op jit(solution)/shard_map/ppermute | solution.py:81
  1311.9 17.5 %collective-permute-done.84 = bf16[256,704]{0,1:T(8,128)(2,1)} collective-permute-done((bf16[256,704]{0,1:T(8,128)(2,1)}, bf16[256,704]{0,1:T(8,128)(2,1)}, u32[]{:S(2)}, u32[]{:S(2)}) %collective-permute-start.84) | collective-permute-done | bytes 360480 | tf_op jit(solution)/shard_map/ppermute | solution.py:81
  (721 shorter events, 690.9 us)
Async XLA Ops:
  101.1 1154.4 %all-reduce.3.cloned.1.call-start = ((), (), s32[]{:S(2)}) async-start(), calls=%async_computation.5 | async-start | bytes 3670016 | tf_op jit(solution)/shard_map/psum | solution.py:881
  220.4 106.7 %collective-permute-start.40 = (bf16[3,256,512]{2,1,0:T(8,128)(2,1)S(1)}, bf16[3,256,512]{2,1,0:T(8,128)(2,1)S(1)}, u32[]{:S(2)}, u32[]{:S(2)}) collective-permute-start(bf16[3,256,512]{2,1,0:T(8,128)(2,1)S(1)} %get-tuple-element.247), channel_id=1, source_target_pairs={{0,4},{1,5},{2,6},{3,7},{4,0},{5,1},{6,2},{7,3},{8,12},{9,13},{10,... | collective-permute-start | bytes 2359304 | tf_op jit(solution)/shard_map/ppermute | solution.py:81
  221.8 106.7 %collective-permute-start.38 = (bf16[3,256,512]{2,1,0:T(8,128)(2,1)S(1)}, bf16[3,256,512]{2,1,0:T(8,128)(2,1)}, u32[]{:S(2)}, u32[]{:S(2)}) collective-permute-start(bf16[3,256,512]{2,1,0:T(8,128)(2,1)S(1)} %get-tuple-element.248), channel_id=1, source_target_pairs={{0,2},{1,3},{2,0},{3,1},{4,6},{5,7},{6,4},{7,5},{8,10},{9,11},{10,... | collective-permute-start | bytes 2359304 | tf_op jit(solution)/shard_map/ppermute | solution.py:81
  282.4 127.1 %collective-permute-start.36 = (bf16[512,2304]{1,0:T(8,128)(2,1)}, bf16[512,2304]{1,0:T(8,128)(2,1)S(1)}, u32[]{:S(2)}, u32[]{:S(2)}) collective-permute-start(bf16[512,2304]{1,0:T(8,128)(2,1)} %pad_maximum_fusion.3.refs_1_), channel_id=1, source_target_pairs={{0,16},{8,24},{16,0},{24,8},{1,17},{9,25},{17,1},{25,9},{2,18},{10... | collective-permute-start | bytes 7077896 | tf_op jit(solution)/shard_map/ppermute | solution.py:77
  294.8 115.2 %collective-permute-start.34 = (bf16[512,2304]{1,0:T(8,128)(2,1)}, bf16[512,2304]{1,0:T(8,128)(2,1)}, u32[]{:S(2)}, u32[]{:S(2)}) collective-permute-start(bf16[512,2304]{1,0:T(8,128)(2,1)} %pad_maximum_fusion.3.refs_1_), channel_id=1, source_target_pairs={{0,8},{8,0},{16,24},{24,16},{1,9},{9,1},{17,25},{25,17},{2,10},{10... | collective-permute-start | bytes 7077896 | tf_op jit(solution)/shard_map/ppermute | solution.py:77
  328.1 85.9 %collective-permute-start.29 = (bf16[512,2304]{1,0:T(8,128)(2,1)}, bf16[512,2304]{1,0:T(8,128)(2,1)}, u32[]{:S(2)}, u32[]{:S(2)}) collective-permute-start(bf16[512,2304]{1,0:T(8,128)(2,1)} %pad_maximum_fusion.1.refs_0_), channel_id=1, source_target_pairs={{0,16},{8,24},{16,0},{24,8},{1,17},{9,25},{17,1},{25,9},{2,18},{10... | collective-permute-start | bytes 7077896 | tf_op jit(solution)/shard_map/ppermute | solution.py:77
  328.5 85.6 %collective-permute-start.27 = (bf16[512,2304]{1,0:T(8,128)(2,1)}, bf16[512,2304]{1,0:T(8,128)(2,1)}, u32[]{:S(2)}, u32[]{:S(2)}) collective-permute-start(bf16[512,2304]{1,0:T(8,128)(2,1)} %pad_maximum_fusion.1.refs_0_), channel_id=1, source_target_pairs={{0,8},{8,0},{16,24},{24,16},{1,9},{9,1},{17,25},{25,17},{2,10},{10... | collective-permute-start | bytes 7077896 | tf_op jit(solution)/shard_map/ppermute | solution.py:77
  442.0 99.6 %collective-permute-start.30 = (bf16[256,2304]{1,0:T(8,128)(2,1)}, bf16[256,2304]{1,0:T(8,128)(2,1)}, u32[]{:S(2)}, u32[]{:S(2)}) collective-permute-start(bf16[256,2304]{1,0:T(8,128)(2,1)} %slice.396), channel_id=1, source_target_pairs={{0,8},{8,0},{16,24},{24,16},{1,9},{9,1},{17,25},{25,17},{2,10},{10... | collective-permute-start | bytes 3538952 | tf_op jit(solution)/shard_map/ppermute | solution.py:77
  442.3 99.3 %collective-permute-start.28 = (bf16[256,2304]{1,0:T(8,128)(2,1)}, bf16[256,2304]{1,0:T(8,128)(2,1)}, u32[]{:S(2)}, u32[]{:S(2)}) collective-permute-start(bf16[256,2304]{1,0:T(8,128)(2,1)} %slice.395), channel_id=1, source_target_pairs={{0,16},{8,24},{16,0},{24,8},{1,17},{9,25},{17,1},{25,9},{2,18},{10... | collective-permute-start | bytes 3538952 | tf_op jit(solution)/shard_map/ppermute | solution.py:77
  610.5 163.3 %collective-permute-start.47 = (bf16[4,6,256,512]{3,2,1,0:T(8,128)(2,1)}, bf16[4,6,256,512]{3,2,1,0:T(8,128)(2,1)}, u32[]{:S(2)}, u32[]{:S(2)}) collective-permute-start(bf16[4,6,256,512]{3,2,1,0:T(8,128)(2,1)} %pick_columns.1), channel_id=1, source_target_pairs={{0,1},{1,0},{2,3},{3,2},{4,5},{5,4},{6,7},{7,6},{8,9},{9,8},{10,11... | collective-permute-start | bytes 18874376 | tf_op jit(solution)/shard_map/ppermute | solution.py:87
  611.1 104.2 %collective-permute-start.52 = (bf16[512,2304]{1,0:T(8,128)(2,1)}, bf16[512,2304]{1,0:T(8,128)(2,1)}, u32[]{:S(2)}, u32[]{:S(2)}) collective-permute-start(bf16[512,2304]{1,0:T(8,128)(2,1)} %get-tuple-element.128), channel_id=1, source_target_pairs={{0,16},{8,24},{16,0},{24,8},{1,17},{9,25},{17,1},{25,9},{2,18},{10... | collective-permute-start | bytes 7077896 | tf_op jit(solution)/shard_map/ppermute | solution.py:77
  627.0 88.3 %collective-permute-start.53 = (bf16[512,2304]{1,0:T(8,128)(2,1)}, bf16[512,2304]{1,0:T(8,128)(2,1)}, u32[]{:S(2)}, u32[]{:S(2)}) collective-permute-start(bf16[512,2304]{1,0:T(8,128)(2,1)} %get-tuple-element.129), channel_id=1, source_target_pairs={{0,24},{8,16},{16,8},{24,0},{1,25},{9,17},{17,9},{25,1},{2,26},{10... | collective-permute-start | bytes 7077896 | tf_op jit(solution)/shard_map/ppermute | solution.py:77
  724.4 110.2 %collective-permute-start.94 = (bf16[128,256]{1,0:T(8,128)(2,1)S(1)}, bf16[128,256]{1,0:T(8,128)(2,1)}, u32[]{:S(2)}, u32[]{:S(2)}) collective-permute-start(bf16[128,256]{1,0:T(8,128)(2,1)S(1)} %slice.560), channel_id=1, source_target_pairs={{0,16},{8,24},{16,0},{24,8},{1,17},{9,25},{17,1},{25,9},{2,18},{10... | collective-permute-start | bytes 196616 | tf_op jit(solution)/shard_map/ppermute | solution.py:77
  746.2 90.2 %collective-permute-start.93 = (bf16[128,256]{1,0:T(8,128)(2,1)S(1)}, bf16[128,256]{1,0:T(8,128)(2,1)}, u32[]{:S(2)}, u32[]{:S(2)}) collective-permute-start(bf16[128,256]{1,0:T(8,128)(2,1)S(1)} %slice.560), channel_id=1, source_target_pairs={{0,8},{8,0},{16,24},{24,16},{1,9},{9,1},{17,25},{25,17},{2,10},{10... | collective-permute-start | bytes 196616 | tf_op jit(solution)/shard_map/ppermute | solution.py:77
  881.9 139.9 %collective-permute-start.57 = (bf16[512,2304]{1,0:T(8,128)(2,1)}, bf16[512,2304]{1,0:T(8,128)(2,1)}, u32[]{:S(2)}, u32[]{:S(2)}) collective-permute-start(bf16[512,2304]{1,0:T(8,128)(2,1)} %get-tuple-element.140), channel_id=1, source_target_pairs={{0,8},{8,0},{16,24},{24,16},{1,9},{9,1},{17,25},{25,17},{2,10},{10... | collective-permute-start | bytes 7077896 | tf_op jit(solution)/shard_map/ppermute | solution.py:77
  882.5 141.2 %collective-permute-start.58 = (bf16[512,2304]{1,0:T(8,128)(2,1)}, bf16[512,2304]{1,0:T(8,128)(2,1)}, u32[]{:S(2)}, u32[]{:S(2)}) collective-permute-start(bf16[512,2304]{1,0:T(8,128)(2,1)} %get-tuple-element.141), channel_id=1, source_target_pairs={{0,16},{8,24},{16,0},{24,8},{1,17},{9,25},{17,1},{25,9},{2,18},{10... | collective-permute-start | bytes 7077896 | tf_op jit(solution)/shard_map/ppermute | solution.py:77
  960.9 337.7 %all-to-all-start.3 = ((bf16[8,16,2048]{2,1,0:T(8,128)(2,1)}), bf16[8,16,2048]{2,1,0:T(8,128)(2,1)S(1)}, u32[]{:S(2)}, u32[]{:S(2)}) async-start(bf16[8,16,2048]{2,1,0:T(8,128)(2,1)} %bitcast.50), calls=%async_computation.3 | async-start | bytes 1048576 | tf_op jit(solution)/shard_map/all_to_all | solution.py:501
  964.4 415.1 %all-gather.2.cloned.1.call-start = ((), (), s32[]{:S(2)}) async-start(), calls=%async_computation.4 | async-start | bytes 1081344 | tf_op jit(solution)/shard_map/all_gather | solution.py:773
  1020.2 179.8 %collective-permute-start.97 = (bf16[6,256,512]{2,1,0:T(8,128)(2,1)}, bf16[6,256,512]{2,1,0:T(8,128)(2,1)S(1)}, u32[]{:S(2)}, u32[]{:S(2)}) collective-permute-start(bf16[6,256,512]{2,1,0:T(8,128)(2,1)} %get-tuple-element.240), channel_id=1, source_target_pairs={{0,4},{1,5},{2,6},{3,7},{4,0},{5,1},{6,2},{7,3},{8,12},{9,13},{10,... | collective-permute-start | bytes 4718600 | tf_op jit(solution)/shard_map/ppermute | solution.py:81
  1021.8 178.3 %collective-permute-start.96 = (bf16[6,256,512]{2,1,0:T(8,128)(2,1)S(1)}, bf16[6,256,512]{2,1,0:T(8,128)(2,1)S(1)}, u32[]{:S(2)}, u32[]{:S(2)}) collective-permute-start(bf16[6,256,512]{2,1,0:T(8,128)(2,1)S(1)} %copy-done.49), channel_id=1, source_target_pairs={{0,2},{1,3},{2,0},{3,1},{4,6},{5,7},{6,4},{7,5},{8,10},{9,11},{10,... | collective-permute-start | bytes 4718600 | tf_op jit(solution)/shard_map/ppermute | solution.py:81
  1028.3 175.3 %collective-permute-start.60 = (bf16[128,2304]{1,0:T(8,128)(2,1)S(1)}, bf16[128,2304]{1,0:T(8,128)(2,1)S(1)}, u32[]{:S(2)}, u32[]{:S(2)}) collective-permute-start(bf16[128,2304]{1,0:T(8,128)(2,1)S(1)} %get-tuple-element.252), channel_id=1, source_target_pairs={{0,2},{1,3},{2,0},{3,1},{4,6},{5,7},{6,4},{7,5},{8,10},{9,11},{10,... | collective-permute-start | bytes 1769480 | tf_op jit(solution)/shard_map/ppermute | solution.py:81
  1028.7 175.3 %collective-permute-start.62 = (bf16[128,2304]{1,0:T(8,128)(2,1)S(1)}, bf16[128,2304]{1,0:T(8,128)(2,1)S(1)}, u32[]{:S(2)}, u32[]{:S(2)}) collective-permute-start(bf16[128,2304]{1,0:T(8,128)(2,1)S(1)} %get-tuple-element.253), channel_id=1, source_target_pairs={{0,6},{1,7},{2,4},{3,5},{4,2},{5,3},{6,0},{7,1},{8,14},{9,15},{10,... | collective-permute-start | bytes 1769480 | tf_op jit(solution)/shard_map/ppermute | solution.py:81
  1059.4 165.9 %collective-permute-start.61 = (bf16[128,2304]{1,0:T(8,128)(2,1)S(1)}, bf16[128,2304]{1,0:T(8,128)(2,1)S(1)}, u32[]{:S(2)}, u32[]{:S(2)}) collective-permute-start(bf16[128,2304]{1,0:T(8,128)(2,1)S(1)} %get-tuple-element.254), channel_id=1, source_target_pairs={{0,4},{1,5},{2,6},{3,7},{4,0},{5,1},{6,2},{7,3},{8,12},{9,13},{10,... | collective-permute-start | bytes 1769480 | tf_op jit(solution)/shard_map/ppermute | solution.py:81
  1204.0 90.8 %collective-permute-start.90 = (bf16[256,512]{0,1:T(8,128)(2,1)}, bf16[256,512]{0,1:T(8,128)(2,1)}, u32[]{:S(2)}, u32[]{:S(2)}) collective-permute-start(bf16[256,512]{0,1:T(8,128)(2,1)} %get-tuple-element.273), channel_id=1, source_target_pairs={{0,2},{1,3},{2,0},{3,1},{4,6},{5,7},{6,4},{7,5},{8,10},{9,11},{10,... | collective-permute-start | bytes 786440 | tf_op jit(solution)/shard_map/ppermute | solution.py:81
  (232 other events, 5523.7 us)
Sparse Core Ops, SparseCore 0:
  954.0 167.3 all-reduce.2
Sparse Core Ops, SparseCore 1:
  1301.2 59.2 all-gather.1
